TPU v7x, 32 devices: a whole 2x2x4 slice. The times are simulated.
32 devices in a mesh: tm: 8 (over z, x), head: 4 (over y, core).
Axes of the slice: x: 2, y: 2, z: 4, core: 2. Of those that a mesh axis runs over, the one named last changes fastest.
Arguments:
- query_rows: float32 [8192, 2048], P('tm', 'head'), may hold values from -0.125 to 0.125
- key_rows: float32 [8192, 2048], P('tm', 'head'), may hold values from -0.125 to 0.125
- value_rows: float32 [8192, 2048], P('tm', 'head'), may hold values from -1.25 to 1.25
- out_grad: float32 [8192, 2048], P('tm', 'head'), may hold values from -1.25 to 1.25
- level_weights: float32 [14, 8192], P(None, 'tm'), may hold values from 0.3 to 3
Outputs:
- query_grad: float32 [8192, 2048], P('tm', 'head')
- key_grad: float32 [8192, 2048], P('tm', 'head')
- value_grad: float32 [8192, 2048], P('tm', 'head')
- weight_grad: float32 [14, 8192], P(None, 'tm')
All inputs are finite; a program needn't handle non-finite values.
Results may differ from a plain program's by a relative error of at most 0.00011.
Values sent between devices are 32-bit elements; how exact they have to be, the bound alone decides.
No kernel may reach another device: no remote copies, remote signals or barrier semaphores. Data moves between devices by JAX's collectives and lax.ppermute only.
A program may use at most 128 MiB of HBM per device.

v0:
```python
import functools

import jax
import jax.numpy as jnp
from jax import lax
from jax.experimental import pallas as pl
from jax.experimental.pallas import tpu as pltpu
from jax.sharding import PartitionSpec as P

DK = 128
C = 128
SUB = 8
NN = (((1,), (0,)), ((), ()))
NT = (((1,), (1,)), ((), ()))
TN = (((0,), (0,)), ((), ()))


def partner(array, axis, stride):
    return lax.ppermute(array, axis, [(i, i ^ 1 << stride) for i in range(lax.axis_size(axis))])


def split(x):
    hi = x.astype(jnp.bfloat16)
    return hi, (x - hi.astype(jnp.float32)).astype(jnp.bfloat16)


def wide(parts):
    return jnp.concatenate(parts, axis=1)


def tall(parts):
    return jnp.concatenate(parts, axis=0)


def dot(a, b, dims):
    return lax.dot_general(a, b, dims, preferred_element_type=jnp.float32)


def halves(x):
    n = x.shape[1] // 2
    return x[:, :n] + x[:, n:]


def nn(a, b):
    right = wide(b)
    return halves(dot(wide(a), tall((right, right)), NN))


def nt(a, b):
    return halves(dot(wide(a), tall((wide((b[0], b[0])), wide((b[1], b[1])))), NT))


def tn(a, b):
    right = wide(b)
    return halves(dot(tall(a), tall((right, right)), TN))


def fold(x):
    return jnp.sum(x.reshape(x.shape[0] // SUB, SUB, x.shape[1]), axis=0)


def level_table():
    s = lax.broadcasted_iota(jnp.int32, (C, C), 0)
    t = lax.broadcasted_iota(jnp.int32, (C, C), 1)
    x = jnp.bitwise_xor(s, t)
    level = jnp.zeros((C, C), jnp.int32)
    for height in range(C.bit_length() - 1):
        level = level + (x >= 1 << height).astype(jnp.int32)
    return jnp.where(s <= t, level, -1)


def state_kernel(first, q_ref, k_ref, v_ref, d_ref, w_ref, s_ref, g_ref):
    frames = q_ref.shape[0]
    vv = wide(split(v_ref[...]))
    kh, kl = split(k_ref[...])
    s_ref[0] = halves(dot(kh, vv, TN) + dot(kl, vv, TN))
    dd = wide(split(d_ref[...]))
    qt = q_ref[...].T
    for level in range(g_ref.shape[0]):
        gh, gl = split(qt * w_ref[first + level : first + level + 1, :])
        g_ref[level, 0] = halves(dot(gh, dd, NN) + dot(gl, dd, NN))


def upper_pairs(chunks):
    heights = chunks.bit_length() - 1
    return [(c, k) for c in range(chunks) for k in range(heights) if c >> k & 1]


def local_kernel(q_ref, k_ref, v_ref, d_ref, w_ref, qg_ref, kg_ref, vg_ref, wg_ref, mt_ref, pr_ref, wc_ref):
    head = pl.program_id(0)
    frames = q_ref.shape[0]
    chunks = frames // C
    heights = chunks.bit_length() - 1
    inner = C.bit_length()
    pairs = upper_pairs(chunks)
    spans = [slice(c * C, (c + 1) * C) for c in range(chunks)]

    @pl.when(head == 0)
    def _():
        table = level_table()
        for c in range(chunks):
            mixing = jnp.zeros((C, C), jnp.float32)
            for level in range(inner):
                mixing = jnp.where(table == level, w_ref[level : level + 1, spans[c]], mixing)
            mt_ref[c] = mixing
        pr_ref[...] = jnp.zeros_like(pr_ref)
        wc_ref[...] = jnp.zeros_like(wc_ref)

    sums = {}
    for c in range(chunks):
        ks = split(k_ref[spans[c], :])
        vs = split(v_ref[spans[c], :])
        if c < chunks - 1:
            sums[c, 0] = tn(ks, vs)
    for k in range(1, heights):
        for b in range(chunks >> k):
            if b << k < chunks - (1 << k):
                sums[b, k] = sums[2 * b, k - 1] + sums[2 * b + 1, k - 1]
    back = {}
    for c in range(chunks):
        q = q_ref[spans[c], :]
        qs, ks = split(q), split(k_ref[spans[c], :])
        vs, ds = split(v_ref[spans[c], :]), split(d_ref[spans[c], :])
        gt = nt(ks, qs)
        et = nt(vs, ds)
        pr_ref[c] += gt * et
        mt = mt_ref[c]
        me, mg = split(mt * et), split(mt * gt)
        kg_ref[spans[c], :] = nn(me, qs)
        vg_ref[spans[c], :] = nn(mg, ds)
        qg = tn(me, ks)
        ups = [k for k in range(heights) if c >> k & 1]
        if ups:
            qt = q.T
            mixed = None
            for k in ups:
                row = w_ref[inner + k : inner + k + 1, spans[c]]
                along = nt(split(sums[(c >> k) - 1, k]), ds)
                wc_ref[pairs.index((c, k))] += fold(qt * along)
                term = row * along
                mixed = term if mixed is None else mixed + term
                grad = nn(split(row * qt), ds)
                key = ((c >> k) - 1, k)
                back[key] = back[key] + grad if key in back else grad
            qg = qg + mixed.T
        qg_ref[spans[c], :] = qg
    for c in range(chunks - 1):
        total = None
        for k in range(heights):
            if not c >> k & 1:
                term = back[c >> k, k]
                total = term if total is None else total + term
        bs = split(total)
        kg_ref[spans[c], :] += nt(split(v_ref[spans[c], :]), bs)
        vg_ref[spans[c], :] += nn(split(k_ref[spans[c], :]), bs)

    @pl.when(head == pl.num_programs(0) - 1)
    def _():
        table = level_table()
        wg_ref[...] = jnp.zeros_like(wg_ref)
        for c in range(chunks):
            product = pr_ref[c]
            for level in range(inner):
                row = jnp.sum(jnp.where(table == level, product, 0.0), axis=0, keepdims=True)
                wg_ref[level : level + 1, spans[c]] = row
        for i, (c, k) in enumerate(pairs):
            wg_ref[inner + k : inner + k + 1, spans[c]] = jnp.sum(wc_ref[i], axis=0, keepdims=True)


def coarse_kernel(first, q_ref, d_ref, w_ref, s_ref, qg_ref, out_ref, wg_ref, wc_ref):
    head = pl.program_id(0)
    frames = q_ref.shape[0]
    levels = s_ref.shape[0]
    states = [split(s_ref[level, 0]) for level in range(levels)]
    left = tall([wide(s) for s in states])

    @pl.when(head == 0)
    def _():
        wc_ref[...] = jnp.zeros_like(wc_ref)

    for c in range(frames // C):
        span = slice(c * C, (c + 1) * C)
        dh, dl = split(d_ref[span, :])
        along = halves(dot(left, tall((wide((dh, dh)), wide((dl, dl)))), NT))
        qt = q_ref[span, :].T
        mixed = None
        for level in range(levels):
            part = along[level * DK : (level + 1) * DK, :]
            wc_ref[level, :, span] += fold(qt * part)
            term = w_ref[first + level : first + level + 1, span] * part
            mixed = term if mixed is None else mixed + term
        out_ref[span, :] = qg_ref[span, :] + mixed.T

    @pl.when(head == pl.num_programs(0) - 1)
    def _():
        wg_ref[...] = jnp.zeros_like(wg_ref)
        for level in range(levels):
            wg_ref[level : level + 1, :] = jnp.sum(wc_ref[level], axis=0, keepdims=True)


def back_kernel(k_ref, v_ref, b_ref, kg_ref, vg_ref, ko_ref, vo_ref):
    bs = split(b_ref[0])
    ko_ref[...] = kg_ref[...] + nt(split(v_ref[...]), bs)
    vo_ref[...] = vg_ref[...] + nn(split(k_ref[...]), bs)


def params():
    return pltpu.CompilerParams(dimension_semantics=("arbitrary",), vmem_limit_bytes=32 * 2**20)


def local(query_rows, key_rows, value_rows, out_grad, level_weights):
    frames, width = query_rows.shape
    heads = width // DK
    levels = level_weights.shape[0]
    fine = frames.bit_length()
    device_levels = levels - fine
    f32 = jnp.float32
    column = pl.BlockSpec((frames, DK), lambda h: (0, h))
    weights = pl.BlockSpec((levels, frames), lambda h: (0, 0))
    state = pl.BlockSpec((1, DK, DK), lambda h: (h, 0, 0))
    stack = pl.BlockSpec((device_levels, 1, DK, DK), lambda h: (0, h, 0, 0))
    big = jax.ShapeDtypeStruct((frames, width), f32)
    fine_rows = -(-fine // SUB) * SUB
    coarse_rows = -(-device_levels // SUB) * SUB
    chunks = frames // C

    states, state_grads = pl.pallas_call(
        functools.partial(state_kernel, fine),
        grid=(heads,),
        in_specs=[column] * 4 + [weights],
        out_specs=[state, stack],
        out_shape=[
            jax.ShapeDtypeStruct((heads, DK, DK), f32),
            jax.ShapeDtypeStruct((device_levels, heads, DK, DK), f32),
        ],
        compiler_params=params(),
        name="states",
    )(query_rows, key_rows, value_rows, out_grad, level_weights)

    q_local, k_local, v_local, w_fine = pl.pallas_call(
        local_kernel,
        grid=(heads,),
        in_specs=[column] * 4 + [weights],
        out_specs=[column] * 3 + [pl.BlockSpec((fine_rows, frames), lambda h: (0, 0))],
        out_shape=[big] * 3 + [jax.ShapeDtypeStruct((fine_rows, frames), f32)],
        scratch_shapes=[
            pltpu.VMEM((chunks, C, C), f32),
            pltpu.VMEM((chunks, C, C), f32),
            pltpu.VMEM((max(1, len(upper_pairs(chunks))), SUB, C), f32),
        ],
        compiler_params=params(),
        name="inside",
    )(query_rows, key_rows, value_rows, out_grad, level_weights)

    device = lax.axis_index("tm")
    block = states
    found = []
    for height in range(device_levels):
        other = partner(block, "tm", height)
        upper = jnp.bitwise_and(jnp.right_shift(device, height), 1) == 1
        found.append(jnp.where(upper, other, jnp.float32(0.0)))
        block = block + other
    sibling = jnp.stack(found)
    upper = jnp.bitwise_and(jnp.right_shift(device, jnp.arange(device_levels)), 1) == 1
    carried = state_grads
    state_back = jnp.zeros_like(states)
    for height in range(device_levels):
        other = partner(carried[height:], "tm", height)
        lower = jnp.bitwise_and(jnp.right_shift(device, height), 1) == 0
        state_back = state_back + jnp.where(lower, other[0], jnp.float32(0.0))
        carried = jnp.concatenate([carried[:height], carried[height:] + other], axis=0)

    q_total, w_coarse = pl.pallas_call(
        functools.partial(coarse_kernel, fine),
        grid=(heads,),
        in_specs=[column] * 2 + [weights, stack, column],
        out_specs=[column, pl.BlockSpec((coarse_rows, frames), lambda h: (0, 0))],
        out_shape=[big, jax.ShapeDtypeStruct((coarse_rows, frames), f32)],
        scratch_shapes=[pltpu.VMEM((device_levels, SUB, frames), f32)],
        input_output_aliases={4: 0},
        compiler_params=params(),
        name="coarse",
    )(query_rows, out_grad, level_weights, sibling, q_local)

    weight_terms = jnp.concatenate([w_fine[:fine], w_coarse[:device_levels]], axis=0)
    weight_grad = lax.psum(weight_terms, "head")

    k_total, v_total = pl.pallas_call(
        back_kernel,
        grid=(heads,),
        in_specs=[column] * 2 + [state, column, column],
        out_specs=[column] * 2,
        out_shape=[big] * 2,
        input_output_aliases={3: 0, 4: 1},
        compiler_params=params(),
        name="back",
    )(key_rows, value_rows, state_back, k_local, v_local)
    return (q_total, k_total, v_total, weight_grad)


def solution(mesh):
    in_specs = (P("tm", "head"), P("tm", "head"), P("tm", "head"), P("tm", "head"), P(None, "tm"))
    out_specs = (P("tm", "head"), P("tm", "head"), P("tm", "head"), P(None, "tm"))
    return jax.shard_map(local, mesh=mesh, in_specs=in_specs, out_specs=out_specs, check_vma=False)
```

profile of v0, /device:TPU:1, one launch (start us, length us, event | category | flops | bytes accessed | tf_op | source)
XLA Modules:
  0.0 106.3 jit_solution(12508515239566575099)
XLA Ops:
  0.6 0.0 copy-start
  0.6 1.6 %copy-done = f32[1024,512]{1,0:T(8,128)S(1)} copy-done((f32[1024,512]{1,0:T(8,128)S(1)}, f32[1024,512]{1,0:T(8,128)}, u32[]{:S(2)}) %copy-start) | copy-done | bytes 2097176
  2.2 0.0 copy-start.2
  2.2 1.6 %copy-done.2 = f32[1024,512]{1,0:T(8,128)S(1)} copy-done((f32[1024,512]{1,0:T(8,128)S(1)}, f32[1024,512]{1,0:T(8,128)}, u32[]{:S(2)}) %copy-start.2) | copy-done | bytes 2097176
  3.8 0.0 copy-start.4
  3.8 1.6 %copy-done.4 = f32[1024,512]{1,0:T(8,128)S(1)} copy-done((f32[1024,512]{1,0:T(8,128)S(1)}, f32[1024,512]{1,0:T(8,128)}, u32[]{:S(2)}) %copy-start.4) | copy-done | bytes 2097176
  5.4 0.0 copy-start.7
  5.4 1.6 %copy-done.7 = f32[1024,512]{1,0:T(8,128)S(1)} copy-done((f32[1024,512]{1,0:T(8,128)S(1)}, f32[1024,512]{1,0:T(8,128)}, u32[]{:S(2)}) %copy-start.7) | copy-done | bytes 2097176
  7.0 0.0 copy-start.10
  7.0 0.8 copy-done.10
  7.8 5.0 %states.1 = (f32[4,128,128]{2,1,0:T(8,128)S(1)}, f32[3,4,128,128]{3,2,1,0:T(8,128)S(1)}) custom-call(f32[1024,512]{1,0:T(8,128)S(1)} %copy-done, f32[1024,512]{1,0:T(8,128)S(1)} %copy-done.4, f32[1024,512]{1,0:T(8,128)S(1)} %copy-done.7, f32[1024,512]{1,0:T(8,128)S(1)} %copy-done.2, f32[14,1024]{1,0:T(8,128)S(1)} %copy-done.10), custom_call_target="tpu_custom_call" | custom-call | tf_op jit(solution)/shard_map/states/pallas_call | solution.py:227
  12.8 0.0 copy-start.1
  12.8 0.0 copy-start.11
  12.8 2.1 %collective-permute-start.3 = (f32[3,4,128,128]{3,2,1,0:T(8,128)S(1)}, f32[3,4,128,128]{3,2,1,0:T(8,128)}, u32[]{:S(2)}, u32[]{:S(2)}) collective-permute-start(f32[3,4,128,128]{3,2,1,0:T(8,128)S(1)} %get-tuple-element.17), channel_id=1, source_target_pairs={{0,4},{4,0},{8,12},{12,8},{16,20},{20,16},{24,28},{28,24},{1,5},{5... | collective-permute-start | bytes 2359304 | tf_op jit(solution)/shard_map/ppermute | solution.py:19
  14.9 0.1 collective-permute-start
  15.0 22.8 %collective-permute-done = f32[4,128,128]{2,1,0:T(8,128)S(1)} collective-permute-done((f32[4,128,128]{2,1,0:T(8,128)S(1)}, f32[4,128,128]{2,1,0:T(8,128)S(1)}, u32[]{:S(2)}, u32[]{:S(2)}) %collective-permute-start) | collective-permute-done | bytes 262176 | tf_op jit(solution)/shard_map/ppermute | solution.py:19
  37.8 0.7 select_bitcast_fusion.2
  38.5 1.3 %collective-permute-start.1 = (f32[4,128,128]{2,1,0:T(8,128)S(1)}, f32[4,128,128]{2,1,0:T(8,128)S(1)}, u32[]{:S(2)}, u32[]{:S(2)}) collective-permute-start(f32[4,128,128]{2,1,0:T(8,128)S(1)} %get-tuple-element.25), channel_id=1, source_target_pairs={{0,8},{4,12},{8,0},{12,4},{16,24},{20,28},{24,16},{28,20},{1,9},{5... | collective-permute-start | bytes 786440 | tf_op jit(solution)/shard_map/ppermute | solution.py:19
  39.8 0.0 collective-permute-done.3
  39.8 1.1 %slice_add_fusion = f32[2,4,128,128]{3,2,1,0:T(8,128)S(1)} fusion(f32[3,4,128,128]{3,2,1,0:T(8,128)} %collective-permute-done.3, f32[3,4,128,128]{3,2,1,0:T(8,128)S(1)} %get-tuple-element.17), kind=kLoop, calls=%fused_computation.1 | loop fusion | flops 131072 | bytes 1572864 | tf_op jit(solution)/shard_map/add | solution.py:271
  40.9 0.3 collective-permute-start.4
  41.1 4.0 %collective-permute-done.1 = f32[4,128,128]{2,1,0:T(8,128)S(1)} collective-permute-done((f32[4,128,128]{2,1,0:T(8,128)S(1)}, f32[4,128,128]{2,1,0:T(8,128)S(1)}, u32[]{:S(2)}, u32[]{:S(2)}) %collective-permute-start.1) | collective-permute-done | bytes 262176 | tf_op jit(solution)/shard_map/ppermute | solution.py:19
  45.2 2.1 %collective-permute-start.2 = (f32[4,128,128]{2,1,0:T(8,128)S(1)}, f32[4,128,128]{2,1,0:T(8,128)}, u32[]{:S(2)}, u32[]{:S(2)}) collective-permute-start(f32[4,128,128]{2,1,0:T(8,128)S(1)} %get-tuple-element.27), channel_id=1, source_target_pairs={{0,16},{4,20},{8,24},{12,28},{16,0},{20,4},{24,8},{28,12},{1,17},{... | collective-permute-start | bytes 786440 | tf_op jit(solution)/shard_map/ppermute | solution.py:19
  47.2 0.0 copy-done.1
  47.2 0.0 copy-done.11
  47.2 0.0 copy-start.3
  47.2 1.6 %copy-done.3 = f32[1024,512]{1,0:T(8,128)S(1)} copy-done((f32[1024,512]{1,0:T(8,128)S(1)}, f32[1024,512]{1,0:T(8,128)}, u32[]{:S(2)}) %copy-start.3) | copy-done | bytes 2097176
  48.8 0.0 copy-start.5
  48.8 1.6 %copy-done.5 = f32[1024,512]{1,0:T(8,128)S(1)} copy-done((f32[1024,512]{1,0:T(8,128)S(1)}, f32[1024,512]{1,0:T(8,128)}, u32[]{:S(2)}) %copy-start.5) | copy-done | bytes 2097176
  50.4 0.0 copy-start.8
  50.4 1.6 %copy-done.8 = f32[1024,512]{1,0:T(8,128)S(1)} copy-done((f32[1024,512]{1,0:T(8,128)S(1)}, f32[1024,512]{1,0:T(8,128)}, u32[]{:S(2)}) %copy-start.8) | copy-done | bytes 2097176
  52.0 0.0 copy-start.12
  52.0 17.5 %inside.1 = (f32[1024,512]{1,0:T(8,128)}, f32[1024,512]{1,0:T(8,128)}, f32[1024,512]{1,0:T(8,128)}, f32[16,1024]{1,0:T(8,128)S(1)}) custom-call(f32[1024,512]{1,0:T(8,128)S(1)} %copy-done.1, f32[1024,512]{1,0:T(8,128)S(1)} %copy-done.5, f32[1024,512]{1,0:T(8,128)S(1)} %copy-done.8, f32[1024,512]{1,0:T(8,128)S(1)} %copy-done.3, f32[14,1024]{1,0:T(8,128)S(1)} %copy-done.11), custom_call_target="tpu_custom_call" | custom-call | tf_op jit(solution)/shard_map/inside/pallas_call | solution.py:240
  69.5 0.0 collective-permute-done.2
  69.5 0.0 collective-permute-done.4
  69.5 1.7 %slice_add_fusion.1 = f32[1,4,128,128]{3,2,1,0:T(8,128)} fusion(f32[2,4,128,128]{3,2,1,0:T(8,128)} %collective-permute-done.4, f32[2,4,128,128]{3,2,1,0:T(8,128)S(1)} %slice_add_fusion), kind=kLoop, calls=%fused_computation.2 | loop fusion | flops 65536 | bytes 786432 | tf_op jit(solution)/shard_map/add | solution.py:271
  71.2 1.3 %collective-permute-start.5 = (f32[1,4,128,128]{3,2,1,0:T(8,128)}, f32[1,4,128,128]{3,2,1,0:T(8,128)S(1)}, u32[]{:S(2)}, u32[]{:S(2)}) collective-permute-start(f32[1,4,128,128]{3,2,1,0:T(8,128)} %slice_add_fusion.1), channel_id=1, source_target_pairs={{0,16},{4,20},{8,24},{12,28},{16,0},{20,4},{24,8},{28,12},{1,17},{... | collective-permute-start | bytes 786440 | tf_op jit(solution)/shard_map/ppermute | solution.py:19
  72.5 0.0 copy-done.12
  72.6 0.1 pad_maximum_fusion.s_ref
  72.6 5.7 %coarse.1 = (f32[1024,512]{1,0:T(8,128)}, f32[8,1024]{1,0:T(8,128)S(1)}) custom-call(f32[1024,512]{1,0:T(8,128)S(1)} %copy-done.1, f32[1024,512]{1,0:T(8,128)S(1)} %copy-done.3, f32[14,1024]{1,0:T(8,128)S(1)} %copy-done.11, f32[3,4,128,128]{3,2,1,0:T(8,128)S(1)} %pad_maximum_fusion.s_ref, ...), custom_call_target="tpu_custom_call", output_to_operand_aliasing={{0}: (4, {})} | custom-call | tf_op jit(solution)/shard_map/coarse/pallas_call | solution.py:273
  78.3 18.1 %psum.7 = f32[14,1024]{1,0:T(8,128)} all-reduce(f32[14,1024]{1,0:T(8,128)S(1)} %pad_maximum_fusion.1), channel_id=1, replica_groups=mesh['tm'=8,'head'=4] {'head'}, use_global_device_ids=true, to_apply=%region_0.1 | all-reduce | flops 14336 | bytes 114688 | tf_op jit(solution)/shard_map/psum | solution.py:286
  96.4 0.0 collective-permute-done.5
  96.4 1.1 %fusion.2.b_ref = f32[4,128,128]{2,1,0:T(8,128)S(1)} fusion(f32[2,4,128,128]{3,2,1,0:T(8,128)} %collective-permute-done.4, f32[3,4,128,128]{3,2,1,0:T(8,128)} %collective-permute-done.3, f32[1,4,128,128]{3,2,1,0:T(8,128)S(1)} %collective-permute-done.5, pred[]{:T(512)S(6)} %eq.23, pred[]{:T(512)S(6)} %eq.22, pred[]{:T(512)S(6)} %eq.21), kind=kLoop, calls=%fused_computation.6 | loop fusion | flops 327680 | bytes 1048579 | tf_op jit(solution)/shard_map/add | solution.py:270
  97.5 0.0 copy-start.6
  97.5 1.6 %copy-done.6 = f32[1024,512]{1,0:T(8,128)S(1)} copy-done((f32[1024,512]{1,0:T(8,128)S(1)}, f32[1024,512]{1,0:T(8,128)}, u32[]{:S(2)}) %copy-start.6) | copy-done | bytes 2097176
  99.1 0.0 copy-start.9
  99.1 1.6 %copy-done.9 = f32[1024,512]{1,0:T(8,128)S(1)} copy-done((f32[1024,512]{1,0:T(8,128)S(1)}, f32[1024,512]{1,0:T(8,128)}, u32[]{:S(2)}) %copy-start.9) | copy-done | bytes 2097176
  100.7 5.6 %back.1 = (f32[1024,512]{1,0:T(8,128)}, f32[1024,512]{1,0:T(8,128)}) custom-call(f32[1024,512]{1,0:T(8,128)S(1)} %copy-done.6, f32[1024,512]{1,0:T(8,128)S(1)} %copy-done.9, f32[4,128,128]{2,1,0:T(8,128)S(1)} %fusion.2.b_ref, f32[1024,512]{1,0:T(8,128)} %get-tuple-element.18.kg_ref, ...), custom_call_target="tpu_custom_call", output_to_operand_aliasing={{0}: (3, {}), {1}: (4, {})} | custom-call | tf_op jit(solution)/shard_map/back/pallas_call | solution.py:288
  (4 shorter events, 0.1 us)
Async XLA Ops:
  0.6 1.6 %copy-start = (f32[1024,512]{1,0:T(8,128)S(1)}, f32[1024,512]{1,0:T(8,128)}, u32[]{:S(2)}) copy-start(f32[1024,512]{1,0:T(8,128)} %q_ref.5) | copy-start | bytes 6291460
  2.2 1.6 %copy-start.2 = (f32[1024,512]{1,0:T(8,128)S(1)}, f32[1024,512]{1,0:T(8,128)}, u32[]{:S(2)}) copy-start(f32[1024,512]{1,0:T(8,128)} %d_ref.5) | copy-start | bytes 6291460
  3.8 1.6 %copy-start.4 = (f32[1024,512]{1,0:T(8,128)S(1)}, f32[1024,512]{1,0:T(8,128)}, u32[]{:S(2)}) copy-start(f32[1024,512]{1,0:T(8,128)} %k_ref.5) | copy-start | bytes 6291460
  5.4 1.6 %copy-start.7 = (f32[1024,512]{1,0:T(8,128)S(1)}, f32[1024,512]{1,0:T(8,128)}, u32[]{:S(2)}) copy-start(f32[1024,512]{1,0:T(8,128)} %v_ref.5) | copy-start | bytes 6291460
  7.0 0.8 copy-start.10
  12.8 34.4 %copy-start.1 = (f32[1024,512]{1,0:T(8,128)S(1)}, f32[1024,512]{1,0:T(8,128)}, u32[]{:S(2)}) copy-start(f32[1024,512]{1,0:T(8,128)} %q_ref.5) | copy-start | bytes 6291460
  12.8 34.4 %copy-start.11 = (f32[14,1024]{1,0:T(8,128)S(1)}, f32[14,1024]{1,0:T(8,128)}, u32[]{:S(2)}) copy-start(f32[14,1024]{1,0:T(8,128)} %w_ref.5) | copy-start | bytes 172036
  12.8 27.0 %collective-permute-start.3 = (f32[3,4,128,128]{3,2,1,0:T(8,128)S(1)}, f32[3,4,128,128]{3,2,1,0:T(8,128)}, u32[]{:S(2)}, u32[]{:S(2)}) collective-permute-start(f32[3,4,128,128]{3,2,1,0:T(8,128)S(1)} %get-tuple-element.17), channel_id=1, source_target_pairs={{0,4},{4,0},{8,12},{12,8},{16,20},{20,16},{24,28},{28,24},{1,5},{5... | collective-permute-start | bytes 2359304 | tf_op jit(solution)/shard_map/ppermute | solution.py:19
  14.9 22.9 %collective-permute-start = (f32[4,128,128]{2,1,0:T(8,128)S(1)}, f32[4,128,128]{2,1,0:T(8,128)S(1)}, u32[]{:S(2)}, u32[]{:S(2)}) collective-permute-start(f32[4,128,128]{2,1,0:T(8,128)S(1)} %get-tuple-element.14), channel_id=1, source_target_pairs={{0,4},{4,0},{8,12},{12,8},{16,20},{20,16},{24,28},{28,24},{1,5},{5... | collective-permute-start | bytes 786440 | tf_op jit(solution)/shard_map/ppermute | solution.py:19
  38.5 6.6 %collective-permute-start.1 = (f32[4,128,128]{2,1,0:T(8,128)S(1)}, f32[4,128,128]{2,1,0:T(8,128)S(1)}, u32[]{:S(2)}, u32[]{:S(2)}) collective-permute-start(f32[4,128,128]{2,1,0:T(8,128)S(1)} %get-tuple-element.25), channel_id=1, source_target_pairs={{0,8},{4,12},{8,0},{12,4},{16,24},{20,28},{24,16},{28,20},{1,9},{5... | collective-permute-start | bytes 786440 | tf_op jit(solution)/shard_map/ppermute | solution.py:19
  40.9 28.7 %collective-permute-start.4 = (f32[2,4,128,128]{3,2,1,0:T(8,128)S(1)}, f32[2,4,128,128]{3,2,1,0:T(8,128)}, u32[]{:S(2)}, u32[]{:S(2)}) collective-permute-start(f32[2,4,128,128]{3,2,1,0:T(8,128)S(1)} %slice_add_fusion), channel_id=1, source_target_pairs={{0,8},{4,12},{8,0},{12,4},{16,24},{20,28},{24,16},{28,20},{1,9},{5... | collective-permute-start | bytes 1572872 | tf_op jit(solution)/shard_map/ppermute | solution.py:19
  45.2 24.3 %collective-permute-start.2 = (f32[4,128,128]{2,1,0:T(8,128)S(1)}, f32[4,128,128]{2,1,0:T(8,128)}, u32[]{:S(2)}, u32[]{:S(2)}) collective-permute-start(f32[4,128,128]{2,1,0:T(8,128)S(1)} %get-tuple-element.27), channel_id=1, source_target_pairs={{0,16},{4,20},{8,24},{12,28},{16,0},{20,4},{24,8},{28,12},{1,17},{... | collective-permute-start | bytes 786440 | tf_op jit(solution)/shard_map/ppermute | solution.py:19
  47.2 1.6 %copy-start.3 = (f32[1024,512]{1,0:T(8,128)S(1)}, f32[1024,512]{1,0:T(8,128)}, u32[]{:S(2)}) copy-start(f32[1024,512]{1,0:T(8,128)} %d_ref.5) | copy-start | bytes 6291460
  48.8 1.6 %copy-start.5 = (f32[1024,512]{1,0:T(8,128)S(1)}, f32[1024,512]{1,0:T(8,128)}, u32[]{:S(2)}) copy-start(f32[1024,512]{1,0:T(8,128)} %k_ref.5) | copy-start | bytes 6291460
  50.4 1.6 %copy-start.8 = (f32[1024,512]{1,0:T(8,128)S(1)}, f32[1024,512]{1,0:T(8,128)}, u32[]{:S(2)}) copy-start(f32[1024,512]{1,0:T(8,128)} %v_ref.5) | copy-start | bytes 6291460
  52.0 20.5 %copy-start.12 = (f32[1,4,128,128]{3,2,1,0:T(8,128)S(1)}, f32[1,4,128,128]{3,2,1,0:T(8,128)}, u32[]{:S(2)}) copy-start(f32[1,4,128,128]{3,2,1,0:T(8,128)} %get-tuple-element.24) | copy-start | bytes 786436
  71.2 25.2 %collective-permute-start.5 = (f32[1,4,128,128]{3,2,1,0:T(8,128)}, f32[1,4,128,128]{3,2,1,0:T(8,128)S(1)}, u32[]{:S(2)}, u32[]{:S(2)}) collective-permute-start(f32[1,4,128,128]{3,2,1,0:T(8,128)} %slice_add_fusion.1), channel_id=1, source_target_pairs={{0,16},{4,20},{8,24},{12,28},{16,0},{20,4},{24,8},{28,12},{1,17},{... | collective-permute-start | bytes 786440 | tf_op jit(solution)/shard_map/ppermute | solution.py:19
  97.5 1.6 %copy-start.6 = (f32[1024,512]{1,0:T(8,128)S(1)}, f32[1024,512]{1,0:T(8,128)}, u32[]{:S(2)}) copy-start(f32[1024,512]{1,0:T(8,128)} %k_ref.5) | copy-start | bytes 6291460
  99.1 1.6 %copy-start.9 = (f32[1024,512]{1,0:T(8,128)S(1)}, f32[1024,512]{1,0:T(8,128)}, u32[]{:S(2)}) copy-start(f32[1024,512]{1,0:T(8,128)} %v_ref.5) | copy-start | bytes 6291460
where the time goes:
time: 107 us; the launch traced here: 106 us
  Pallas kernels  33.7 us (31%)
  waiting for transfers between devices  26.8 us (25%)
  blocking collectives  18.1 us (17%)
  local copies, waits for them, and re-layouts  15.2 us (14%)
  starting transfers between devices  7.09 us (7%)
  other arithmetic  4.71 us (4%)
    ppermute x6, waiting for transfers between devices, partner(): lax.ppermute(array, axis, [(i, i ^ 1 << stride) for i in range(lax.axis_s...  26.8 us
    psum x1, blocking collectives, local(): weight_grad = lax.psum(weight_terms, 'head')  18.1 us
    pallas_call x1, Pallas kernels, local(): pl.pallas_call(local_kernel, grid=(heads,), in_specs=[column] * 4 + [weig...  17.5 us
    unnamed x26, local copies, waits for them, and re-layouts  15.2 us
    ppermute x6, starting transfers between devices, partner(): lax.ppermute(array, axis, [(i, i ^ 1 << stride) for i in range(lax.axis_s...  7.09 us
    pallas_call x1, Pallas kernels, local(): pl.pallas_call(functools.partial(coarse_kernel, fine), grid=(heads,), in_...  5.69 us
    pallas_call x1, Pallas kernels, local(): pl.pallas_call(back_kernel, grid=(heads,), in_specs=[column] * 2 + [state...  5.58 us
    pallas_call x1, Pallas kernels, local(): pl.pallas_call(functools.partial(state_kernel, fine), grid=(heads,), in_s...  4.95 us
  transfers between devices with their start and end apart: 6, of which 2 were waited for; matrix products, arithmetic and copies ran while one was open for 2% of the time, Pallas kernels for 22%

commit v1 on v0

v1 whole, which is shorter than its diff:
```python
import functools

import jax
import jax.numpy as jnp
from jax import lax
from jax.experimental import pallas as pl
from jax.experimental.pallas import tpu as pltpu
from jax.sharding import PartitionSpec as P


DK = 128
C = 128
SUB = 8
NN = (((1,), (0,)), ((), ()))
NT = (((1,), (1,)), ((), ()))
TN = (((0,), (0,)), ((), ()))


def partner(array, axis, stride):
    return lax.ppermute(array, axis, [(i, i ^ 1 << stride) for i in range(lax.axis_size(axis))])


def split(x):
    hi = x.astype(jnp.bfloat16)
    return hi, (x - hi.astype(jnp.float32)).astype(jnp.bfloat16)


def wide(parts):
    return jnp.concatenate(parts, axis=1)


def tall(parts):
    return jnp.concatenate(parts, axis=0)


def dot(a, b, dims):
    return lax.dot_general(a, b, dims, preferred_element_type=jnp.float32)


def halves(x):
    n = x.shape[1] // 2
    return x[:, :n] + x[:, n:]


def nn(a, b):
    right = wide(b)
    return halves(dot(wide(a), tall((right, right)), NN))


def nt(a, b):
    return halves(dot(wide(a), tall((wide((b[0], b[0])), wide((b[1], b[1])))), NT))


def tn(a, b):
    right = wide(b)
    return halves(dot(tall(a), tall((right, right)), TN))


def fold(x):
    return jnp.sum(x.reshape(x.shape[0] // SUB, SUB, x.shape[1]), axis=0)


def level_table():
    s = lax.broadcasted_iota(jnp.int32, (C, C), 0)
    t = lax.broadcasted_iota(jnp.int32, (C, C), 1)
    x = jnp.bitwise_xor(s, t)
    level = jnp.zeros((C, C), jnp.int32)
    for height in range(C.bit_length() - 1):
        level = level + (x >= 1 << height).astype(jnp.int32)
    return jnp.where(s <= t, level, -1)


def head_order(i, own, heads):
    return (i + (1 - own) * (heads // 2)) % heads


def state_kernel(first, bits_ref, q_ref, k_ref, v_ref, d_ref, w_ref, near_ref, send_ref, keep_ref, mix_ref):
    step = pl.program_id(0)
    half = pl.num_programs(0) // 2
    levels = send_ref.shape[0] + 1
    chunks, inner = mix_ref.shape[0], C.bit_length()

    @pl.when(step == 0)
    def _():
        table = level_table()
        for c in range(chunks):
            mixing = jnp.zeros((C, C), jnp.float32)
            for level in range(inner):
                mixing = jnp.where(table == level, w_ref[level : level + 1, c * C : (c + 1) * C], mixing)
            mix_ref[c] = mixing

    vv = wide(split(v_ref[...]))
    kh, kl = split(k_ref[...])
    state = halves(dot(kh, vv, TN) + dot(kl, vv, TN))
    dd = wide(split(d_ref[...]))
    qt = q_ref[...].T
    for level in range(levels):
        gh, gl = split(qt * w_ref[first + level : first + level + 1, :])
        grad = halves(dot(gh, dd, NN) + dot(gl, dd, NN))
        moved = jnp.where(bits_ref[level] == 1, grad, state)
        if level == 0:
            near_ref[0] = moved
        else:

            @pl.when(step < half)
            def _(level=level, moved=moved):
                send_ref[level - 1, 0] = moved

            @pl.when(step >= half)
            def _(level=level, moved=moved):
                keep_ref[level - 1, 0] = moved


def upper_pairs(chunks):
    heights = chunks.bit_length() - 1
    return [(c, k) for c in range(chunks) for k in range(heights) if c >> k & 1]


def local_kernel(start, last, *refs):
    q_ref, k_ref, v_ref, d_ref, w_ref, mix_ref = refs[:6]
    if start:
        qg_ref, kg_ref, vg_ref, pr_ref, wc_ref = refs[6:11]
    else:
        old_pr, old_wc = refs[9:11]
        qg_ref, kg_ref, vg_ref, pr_ref, wc_ref = refs[11:16]
    head = pl.program_id(0)
    frames = q_ref.shape[0]
    chunks = frames // C
    heights = chunks.bit_length() - 1
    inner = C.bit_length()
    pairs = upper_pairs(chunks)
    spans = [slice(c * C, (c + 1) * C) for c in range(chunks)]

    @pl.when(head == 0)
    def _():
        pr_ref[...] = jnp.zeros_like(pr_ref) if start else old_pr[...]
        wc_ref[...] = jnp.zeros_like(wc_ref) if start else old_wc[...]

    sums = {}
    for c in range(chunks):
        ks = split(k_ref[spans[c], :])
        vs = split(v_ref[spans[c], :])
        if c < chunks - 1:
            sums[c, 0] = tn(ks, vs)
    for k in range(1, heights):
        for b in range(chunks >> k):
            if b << k < chunks - (1 << k):
                sums[b, k] = sums[2 * b, k - 1] + sums[2 * b + 1, k - 1]
    back = {}
    for c in range(chunks):
        q = q_ref[spans[c], :]
        qs, ks = split(q), split(k_ref[spans[c], :])
        vs, ds = split(v_ref[spans[c], :]), split(d_ref[spans[c], :])
        gt = nt(ks, qs)
        et = nt(vs, ds)
        pr_ref[c] += gt * et
        mt = mix_ref[c]
        me, mg = split(mt * et), split(mt * gt)
        kg_ref[spans[c], :] = nn(me, qs)
        vg_ref[spans[c], :] = nn(mg, ds)
        qg = tn(me, ks)
        ups = [k for k in range(heights) if c >> k & 1]
        if ups:
            qt = q.T
            mixed = None
            for k in ups:
                row = w_ref[inner + k : inner + k + 1, spans[c]]
                along = nt(split(sums[(c >> k) - 1, k]), ds)
                wc_ref[pairs.index((c, k))] += fold(qt * along)
                term = row * along
                mixed = term if mixed is None else mixed + term
                grad = nn(split(row * qt), ds)
                key = ((c >> k) - 1, k)
                back[key] = back[key] + grad if key in back else grad
            qg = qg + mixed.T
        qg_ref[spans[c], :] = qg
    for c in range(chunks - 1):
        total = None
        for k in range(heights):
            if not c >> k & 1:
                term = back[c >> k, k]
                total = term if total is None else total + term
        bs = split(total)
        kg_ref[spans[c], :] += nt(split(v_ref[spans[c], :]), bs)
        vg_ref[spans[c], :] += nn(split(k_ref[spans[c], :]), bs)

    if last:
        wg_ref = refs[-1]

        @pl.when(head == pl.num_programs(0) - 1)
        def _():
            table = level_table()
            wg_ref[...] = jnp.zeros_like(wg_ref)
            for c in range(chunks):
                product = pr_ref[c]
                for level in range(inner):
                    row = jnp.sum(jnp.where(table == level, product, 0.0), axis=0, keepdims=True)
                    wg_ref[level : level + 1, spans[c]] = row
            for i, (c, k) in enumerate(pairs):
                wg_ref[inner + k : inner + k + 1, spans[c]] = jnp.sum(wc_ref[i], axis=0, keepdims=True)


def received(refs, levels):
    step = pl.program_id(0)
    half = pl.num_programs(0) // 2
    found = [refs[0][0]]
    for level in range(1, levels):
        found.append(jnp.where(step < half, refs[2 * level - 1][0], refs[2 * level][0]))
    return found


def coarse_kernel(first, levels, bits_ref, *refs):
    q_ref, d_ref, w_ref = refs[:3]
    arrived = refs[3 : 2 + 2 * levels]
    qg_ref, out_ref, wg_ref, wc_ref = refs[2 + 2 * levels :]
    step = pl.program_id(0)
    frames = q_ref.shape[0]
    states = []
    for level, state in enumerate(received(arrived, levels)):
        states.append(split(jnp.where(bits_ref[level] == 1, state, 0.0)))
    left = tall([wide(s) for s in states])

    @pl.when(step == 0)
    def _():
        wc_ref[...] = jnp.zeros_like(wc_ref)

    for c in range(frames // C):
        span = slice(c * C, (c + 1) * C)
        dh, dl = split(d_ref[span, :])
        along = halves(dot(left, tall((wide((dh, dh)), wide((dl, dl)))), NT))
        qt = q_ref[span, :].T
        mixed = None
        for level in range(levels):
            part = along[level * DK : (level + 1) * DK, :]
            wc_ref[level, :, span] += fold(qt * part)
            term = w_ref[first + level : first + level + 1, span] * part
            mixed = term if mixed is None else mixed + term
        out_ref[span, :] = qg_ref[span, :] + mixed.T

    @pl.when(step == pl.num_programs(0) - 1)
    def _():
        wg_ref[...] = jnp.zeros_like(wg_ref)
        for level in range(levels):
            wg_ref[level : level + 1, :] = jnp.sum(wc_ref[level], axis=0, keepdims=True)


def back_kernel(levels, bits_ref, *refs):
    k_ref, v_ref = refs[:2]
    arrived = refs[2 : 1 + 2 * levels]
    kg_ref, vg_ref, ko_ref, vo_ref = refs[1 + 2 * levels :]
    total = None
    for level, state in enumerate(received(arrived, levels)):
        term = jnp.where(bits_ref[level] == 0, state, 0.0)
        total = term if total is None else total + term
    bs = split(total)
    ko_ref[...] = kg_ref[...] + nt(split(v_ref[...]), bs)
    vo_ref[...] = vg_ref[...] + nn(split(k_ref[...]), bs)


def params(mib):
    return pltpu.CompilerParams(dimension_semantics=("arbitrary",), vmem_limit_bytes=mib * 2**20)


def cost(flops, size):
    return pl.CostEstimate(flops=flops, bytes_accessed=size, transcendentals=0)


def body(query_rows, key_rows, value_rows, out_grad, level_weights):
    frames, width = query_rows.shape
    heads = width // DK
    half = heads // 2
    levels = level_weights.shape[0]
    fine = frames.bit_length()
    device_levels = levels - fine
    far = device_levels - 1
    f32 = jnp.float32
    big = jax.ShapeDtypeStruct((frames, width), f32)
    fine_rows = -(-fine // SUB) * SUB
    coarse_rows = -(-device_levels // SUB) * SUB
    chunks = frames // C
    pairs = max(1, len(upper_pairs(chunks)))
    block = frames * width * 4
    device = lax.axis_index("tm")
    bits = jnp.bitwise_and(jnp.right_shift(device, jnp.arange(device_levels)), 1).astype(jnp.int32)

    def whole(shape):
        return pl.BlockSpec(shape, lambda i, *s: (0,) * len(shape))

    ordered = pl.BlockSpec((frames, DK), lambda i, b: (0, head_order(i, b[0], heads)))
    first_half = lambda i: jnp.minimum(i, half - 1)
    second_half = lambda i: jnp.maximum(i - half, 0)

    near, send, keep, mix = pl.pallas_call(
        functools.partial(state_kernel, fine),
        grid_spec=pltpu.PrefetchScalarGridSpec(
            num_scalar_prefetch=1,
            grid=(heads,),
            in_specs=[ordered] * 4 + [whole((levels, frames))],
            out_specs=[
                pl.BlockSpec((1, DK, DK), lambda i, b: (head_order(i, b[0], heads), 0, 0)),
                pl.BlockSpec((far, 1, DK, DK), lambda i, b: (0, first_half(i), 0, 0)),
                pl.BlockSpec((far, 1, DK, DK), lambda i, b: (0, second_half(i), 0, 0)),
                whole((chunks, C, C)),
            ],
        ),
        out_shape=[
            jax.ShapeDtypeStruct((heads, DK, DK), f32),
            jax.ShapeDtypeStruct((far, half, DK, DK), f32),
            jax.ShapeDtypeStruct((far, half, DK, DK), f32),
            jax.ShapeDtypeStruct((chunks, C, C), f32),
        ],
        compiler_params=params(58),
        cost_estimate=cost(10**9, 4 * block),
        name="states",
    )(bits, query_rows, key_rows, value_rows, out_grad, level_weights)

    local = None
    for piece in range(heads):
        start, last = piece == 0, piece == heads - 1
        column = pl.BlockSpec((frames, DK), lambda i, piece=piece: (0, piece + i))
        anywhere = pl.BlockSpec(memory_space=pl.ANY)
        carry = [whole((chunks, C, C)), whole((pairs, SUB, C))]
        shapes = [big] * 3 + [jax.ShapeDtypeStruct((chunks, C, C), f32), jax.ShapeDtypeStruct((pairs, SUB, C), f32)]
        local = pl.pallas_call(
            functools.partial(local_kernel, start, last),
            grid=(1,),
            in_specs=[column] * 4
            + [whole((levels, frames)), whole((chunks, C, C))]
            + ([] if start else [anywhere] * 3 + carry),
            out_specs=[column] * 3 + carry + ([whole((fine_rows, frames))] if last else []),
            out_shape=shapes + ([jax.ShapeDtypeStruct((fine_rows, frames), f32)] if last else []),
            input_output_aliases={} if start else {6 + i: i for i in range(5)},
            compiler_params=params(58),
            cost_estimate=cost(10**9, 7 * block // heads),
        )(query_rows, key_rows, value_rows, out_grad, level_weights, mix, *(local or []))
    q_local, k_local, v_local, _, _, w_fine = local

    arrived = []
    carried = keep + partner(send, "tm", 0)
    for height in range(1, device_levels):
        other = partner(carried, "tm", height)
        arrived.append(other[0])
        carried = carried[1:] + other[1:]
    states = [partner(near, "tm", 0)]
    for height in range(far):
        states += [partner(arrived[height], "tm", 0), arrived[height]]

    state_specs = [pl.BlockSpec((1, DK, DK), lambda i, b: (head_order(i, b[0], heads), 0, 0))]
    for _ in range(far):
        state_specs.append(pl.BlockSpec((1, DK, DK), lambda i, b: (first_half(i), 0, 0)))
        state_specs.append(pl.BlockSpec((1, DK, DK), lambda i, b: (second_half(i), 0, 0)))

    q_total, w_coarse = pl.pallas_call(
        functools.partial(coarse_kernel, fine, device_levels),
        grid_spec=pltpu.PrefetchScalarGridSpec(
            num_scalar_prefetch=1,
            grid=(heads,),
            in_specs=[ordered] * 2 + [whole((levels, frames))] + state_specs + [ordered],
            out_specs=[ordered, whole((coarse_rows, frames))],
            scratch_shapes=[pltpu.VMEM((device_levels, SUB, frames), f32)],
        ),
        out_shape=[big, jax.ShapeDtypeStruct((coarse_rows, frames), f32)],
        input_output_aliases={4 + len(state_specs): 0},
        compiler_params=params(58),
        cost_estimate=cost(10**9, 4 * block),
        name="coarse",
    )(bits, query_rows, out_grad, level_weights, *states, q_local)

    weight_grad = jnp.concatenate([w_fine[:fine], w_coarse[:device_levels]], axis=0)
    for height in range(lax.axis_size("head").bit_length() - 1):
        weight_grad = weight_grad + partner(weight_grad, "head", height)

    k_total, v_total = pl.pallas_call(
        functools.partial(back_kernel, device_levels),
        grid_spec=pltpu.PrefetchScalarGridSpec(
            num_scalar_prefetch=1,
            grid=(heads,),
            in_specs=[ordered] * 2 + state_specs + [ordered] * 2,
            out_specs=[ordered] * 2,
        ),
        out_shape=[big] * 2,
        input_output_aliases={3 + len(state_specs): 0, 4 + len(state_specs): 1},
        compiler_params=params(58),
        cost_estimate=cost(10**9, 6 * block),
        name="back",
    )(bits, key_rows, value_rows, *states, k_local, v_local)
    return (q_total, k_total, v_total, weight_grad)


def solution(mesh):
    in_specs = (P("tm", "head"), P("tm", "head"), P("tm", "head"), P("tm", "head"), P(None, "tm"))
    out_specs = (P("tm", "head"), P("tm", "head"), P("tm", "head"), P(None, "tm"))
    return jax.shard_map(body, mesh=mesh, in_specs=in_specs, out_specs=out_specs, check_vma=False)
```

time: 107 us -> 79.5 us (0.74)
  blocking collectives: 18.1 us -> 0 us
  Pallas kernels: 33.7 us -> 49.7 us
  waiting for transfers between devices: 26.8 us -> 11.3 us
  local copies, waits for them, and re-layouts: 15.2 us -> 1.53 us
  starting transfers between devices: 7.09 us -> 12.8 us
  other arithmetic: 4.71 us -> 2.26 us
    psum x1 -> x0, blocking collectives: 18.1 us -> none  [local(): weight_grad = lax.psum(weight_terms, 'head')]
    pallas_call x4 -> x7, Pallas kernels: 33.7 us -> 49.7 us  [the longest x4 26 us: body(): pl.pallas_call(functools.partial(local_kernel, start, last), grid=(1,), i...]
    ppermute x6 -> x8, waiting for transfers between devices: 26.8 us -> 11.3 us  [partner(): lax.ppermute(array, axis, [(i, i ^ 1 << stride) for i in range(lax.axis_s...]
    unnamed x26 -> x12, local copies, waits for them, and re-layouts: 15.2 us -> 0.77 us
    ppermute x6 -> x8, starting transfers between devices: 7.09 us -> 12.8 us  [partner(): lax.ppermute(array, axis, [(i, i ^ 1 << stride) for i in range(lax.axis_s...]
    add x3 -> x4, other arithmetic: 3.86 us -> 1.67 us  [the longest x1 0.99 us: body(): carried = keep + partner(send, 'tm', 0)]
  transfers between devices with their start and end apart: 6 -> 8, of which waited for: 2 -> 3; matrix products, arithmetic and copies ran while one was open for 2% -> 0% of each run, Pallas kernels for 22% -> 43%
where the time goes in v1:
time: 79.5 us; the launch traced here: 78.3 us
  Pallas kernels  49.7 us (63%)
  starting transfers between devices  12.8 us (16%)
  waiting for transfers between devices  11.3 us (14%)
  other arithmetic  2.26 us (3%)
  local copies, waits for them, and re-layouts  1.53 us (2%)
    pallas_call x4, Pallas kernels, body(): pl.pallas_call(functools.partial(local_kernel, start, last), grid=(1,), i...  26 us
    ppermute x8, starting transfers between devices, partner(): lax.ppermute(array, axis, [(i, i ^ 1 << stride) for i in range(lax.axis_s...  12.8 us
    ppermute x8, waiting for transfers between devices, partner(): lax.ppermute(array, axis, [(i, i ^ 1 << stride) for i in range(lax.axis_s...  11.3 us
    pallas_call x1, Pallas kernels, body(): pl.pallas_call(functools.partial(state_kernel, fine), grid_spec=pltpu.Pre...  8.97 us
    pallas_call x1, Pallas kernels, body(): pl.pallas_call(functools.partial(back_kernel, device_levels), grid_spec=p...  7.4 us
    pallas_call x1, Pallas kernels, body(): pl.pallas_call(functools.partial(coarse_kernel, fine, device_levels), gri...  7.38 us
  transfers between devices with their start and end apart: 8, of which 3 were waited for; matrix products, arithmetic and copies ran while one was open for 0% of the time, Pallas kernels for 43%

profile of v1, /device:TPU:1, one launch (start us, length us, event | category | flops | bytes accessed | tf_op | source)
XLA Modules:
  0.0 78.3 jit_solution(11732070679222632447)
XLA Ops:
  0.6 0.6 shift-right-arithmetic_and_fusion.bits_ref
  1.2 9.0 %states.1 = (f32[4,128,128]{2,1,0:T(8,128)}, f32[2,2,128,128]{3,2,1,0:T(8,128)}, f32[2,2,128,128]{3,2,1,0:T(8,128)}, f32[8,128,128]{2,1,0:T(8,128)}) custom-call(s32[3]{0:T(128)} %shift-right-arithmetic_and_fusion.bits_ref, f32[1024,512]{1,0:T(8,128)} %refs_0_.10, f32[1024,512]{1,0:T(8,128)} %refs_0_.11, f32[1024,512]{1,0:T(8,128)} %refs_1_.11, ...), custom_call_target="tpu_custom_call" | custom-call | flops 1000000000 | bytes 8388608 | tf_op jit(solution)/shard_map/states/pallas_call | solution.py:293
  10.2 2.1 %collective-permute-start.1 = (f32[2,2,128,128]{3,2,1,0:T(8,128)}, f32[2,2,128,128]{3,2,1,0:T(8,128)S(1)}, u32[]{:S(2)}, u32[]{:S(2)}) collective-permute-start(f32[2,2,128,128]{3,2,1,0:T(8,128)} %get-tuple-element.33), channel_id=1, source_target_pairs={{0,4},{4,0},{8,12},{12,8},{16,20},{20,16},{24,28},{28,24},{1,5},{5... | collective-permute-start | bytes 786440 | tf_op jit(solution)/shard_map/ppermute | solution.py:20
  12.3 6.2 %collective-permute-done.1 = f32[2,2,128,128]{3,2,1,0:T(8,128)S(1)} collective-permute-done((f32[2,2,128,128]{3,2,1,0:T(8,128)}, f32[2,2,128,128]{3,2,1,0:T(8,128)S(1)}, u32[]{:S(2)}, u32[]{:S(2)}) %collective-permute-start.1) | collective-permute-done | bytes 262176 | tf_op jit(solution)/shard_map/ppermute | solution.py:20
  18.5 1.0 %add.12 = f32[2,2,128,128]{3,2,1,0:T(8,128)S(1)} add(f32[2,2,128,128]{3,2,1,0:T(8,128)} %get-tuple-element.32, f32[2,2,128,128]{3,2,1,0:T(8,128)S(1)} %collective-permute-done.1) | non-fusion elementwise | flops 65536 | bytes 786432 | tf_op jit(solution)/shard_map/add | solution.py:339
  19.5 1.3 %collective-permute-start.2 = (f32[2,2,128,128]{3,2,1,0:T(8,128)S(1)}, f32[2,2,128,128]{3,2,1,0:T(8,128)S(1)}, u32[]{:S(2)}, u32[]{:S(2)}) collective-permute-start(f32[2,2,128,128]{3,2,1,0:T(8,128)S(1)} %add.12), channel_id=1, source_target_pairs={{0,8},{4,12},{8,0},{12,4},{16,24},{20,28},{24,16},{28,20},{1,9},{5... | collective-permute-start | bytes 786440 | tf_op jit(solution)/shard_map/ppermute | solution.py:20
  20.8 1.2 %collective-permute-start = (f32[4,128,128]{2,1,0:T(8,128)}, f32[4,128,128]{2,1,0:T(8,128)S(1)}, u32[]{:S(2)}, u32[]{:S(2)}) collective-permute-start(f32[4,128,128]{2,1,0:T(8,128)} %get-tuple-element.31), channel_id=1, source_target_pairs={{0,4},{4,0},{8,12},{12,8},{16,20},{20,16},{24,28},{28,24},{1,5},{5... | collective-permute-start | bytes 786440 | tf_op jit(solution)/shard_map/ppermute | solution.py:20
  22.0 4.1 %collective-permute-done.2 = f32[2,2,128,128]{3,2,1,0:T(8,128)S(1)} collective-permute-done((f32[2,2,128,128]{3,2,1,0:T(8,128)S(1)}, f32[2,2,128,128]{3,2,1,0:T(8,128)S(1)}, u32[]{:S(2)}, u32[]{:S(2)}) %collective-permute-start.2) | collective-permute-done | bytes 262176 | tf_op jit(solution)/shard_map/ppermute | solution.py:20
  26.2 0.0 copy-start
  26.2 2.1 %collective-permute-start.4 = (f32[1,2,128,128]{3,2,1,0:T(8,128)S(1)}, f32[1,2,128,128]{3,2,1,0:T(8,128)S(1)}, u32[]{:S(2)}, u32[]{:S(2)}) collective-permute-start(f32[1,2,128,128]{3,2,1,0:T(8,128)S(1)} %get-tuple-element.58), channel_id=1, source_target_pairs={{0,16},{4,20},{8,24},{12,28},{16,0},{20,4},{24,8},{28,12},{1,17},{... | collective-permute-start | bytes 393224 | tf_op jit(solution)/shard_map/ppermute | solution.py:20
  28.3 6.3 %shard_map.84 = (f32[1024,512]{1,0:T(8,128)}, f32[1024,512]{1,0:T(8,128)}, f32[1024,512]{1,0:T(8,128)}, f32[8,128,128]{2,1,0:T(8,128)}, f32[12,8,128]{2,1,0:T(8,128)}) custom-call(f32[1024,512]{1,0:T(8,128)} %refs_0_.10, f32[1024,512]{1,0:T(8,128)} %refs_0_.11, f32[1024,512]{1,0:T(8,128)} %refs_1_.11, f32[1024,512]{1,0:T(8,128)} %refs_1_.10, ...), custom_call_target="tpu_custom_call" | custom-call | flops 1000000000 | bytes 3670016 | tf_op jit(solution)/shard_map/pallas_call | solution.py:324
  34.5 6.5 %shard_map.85 = (f32[1024,512]{1,0:T(8,128)}, f32[1024,512]{1,0:T(8,128)}, f32[1024,512]{1,0:T(8,128)}, f32[8,128,128]{2,1,0:T(8,128)}, f32[12,8,128]{2,1,0:T(8,128)}) custom-call(f32[1024,512]{1,0:T(8,128)} %refs_0_.10, f32[1024,512]{1,0:T(8,128)} %refs_0_.11, ...), custom_call_target="tpu_custom_call", output_to_operand_aliasing={{0}: (6, {}), {1}: (7, {}), {2}: (8, {}), {3}: (9, {}), {4}... | custom-call | flops 1000000000 | bytes 3670016 | tf_op jit(solution)/shard_map/pallas_call | solution.py:324
  41.0 0.0 copy-done
  41.0 1.2 %collective-permute-start.3 = (f32[2,128,128]{2,1,0:T(8,128)S(1)}, f32[2,128,128]{2,1,0:T(8,128)S(1)}, u32[]{:S(2)}, u32[]{:S(2)}) collective-permute-start(f32[2,128,128]{2,1,0:T(8,128)S(1)} %get-tuple-element.59.refs_5_.refs_4_), channel_id=1, source_target_pairs={{0,4},{4,0},{8,12},{12,8},{16,20},{20,16},{24,28},{28,24},{1,5},{5... | collective-permute-start | bytes 393224 | tf_op jit(solution)/shard_map/ppermute | solution.py:20
  42.2 0.0 collective-permute-done.4
  42.2 0.0 copy-start.2
  42.2 0.3 collective-permute-start.5
  42.5 6.4 %shard_map.86 = (f32[1024,512]{1,0:T(8,128)}, f32[1024,512]{1,0:T(8,128)}, f32[1024,512]{1,0:T(8,128)}, f32[8,128,128]{2,1,0:T(8,128)}, f32[12,8,128]{2,1,0:T(8,128)}) custom-call(f32[1024,512]{1,0:T(8,128)} %refs_0_.10, f32[1024,512]{1,0:T(8,128)} %refs_0_.11, ...), custom_call_target="tpu_custom_call", output_to_operand_aliasing={{0}: (6, {}), {1}: (7, {}), {2}: (8, {}), {3}: (9, {}), {4}... | custom-call | flops 1000000000 | bytes 3670016 | tf_op jit(solution)/shard_map/pallas_call | solution.py:324
  48.9 0.0 copy-done.2
  48.9 6.9 %shard_map.87 = (f32[1024,512]{1,0:T(8,128)}, f32[1024,512]{1,0:T(8,128)}, f32[1024,512]{1,0:T(8,128)}, f32[8,128,128]{2,1,0:T(8,128)}, f32[12,8,128]{2,1,0:T(8,128)}, /*index=5*/f32[16,1024]{1,0:T(8,128)}) custom-call(f32[1024,512]{1,0:T(8,128)} %refs_0_.10, ...), custom_call_target="tpu_custom_call", output_to_operand_aliasing={{0}: (6, {}), {1}: (7, {}), {2}: (8, {}), {3}: (9, {}), {4}... | custom-call | flops 1000000000 | bytes 3670016 | tf_op jit(solution)/shard_map/pallas_call | solution.py:324
  55.7 0.0 collective-permute-done.refs_3_.refs_2_
  55.8 0.0 copy-start.1
  55.8 0.0 collective-permute-done.3.refs_4_.refs_3_
  55.8 0.0 copy-start.3
  55.8 0.0 collective-permute-done.5.refs_6_.refs_5_
  55.8 0.0 copy-start.4
  55.8 0.6 copy-done.1
  56.5 0.1 copy-done.3
  56.5 0.1 copy-done.4
  56.6 0.0 copy-start.5
  56.6 7.4 %coarse.1 = (f32[1024,512]{1,0:T(8,128)}, f32[8,1024]{1,0:T(8,128)}) custom-call(s32[3]{0:T(128)} %shift-right-arithmetic_and_fusion.bits_ref, f32[1024,512]{1,0:T(8,128)} %refs_0_.10, f32[1024,512]{1,0:T(8,128)} %refs_1_.10, f32[14,1024]{1,0:T(8,128)} %refs_2_.9, f32[4,128,128]{2,1,0:T(8,128)} %copy-done.1, ...), custom_call_target="tpu_custom_call", output_to_operand_aliasing={{0}: (9, {})} | custom-call | flops 1000000000 | bytes 8388608 | tf_op jit(solution)/shard_map/coarse/pallas_call | solution.py:353
  63.9 0.8 slice.19
  64.7 0.0 copy-done.5
  64.7 3.3 %collective-permute-start.6 = (f32[14,1024]{1,0:T(8,128)S(1)}, f32[14,1024]{1,0:T(8,128)S(1)}, u32[]{:S(2)}, u32[]{:S(2)}) collective-permute-start(f32[14,1024]{1,0:T(8,128)S(1)} %pad_maximum_fusion), channel_id=1, source_target_pairs={{0,1},{1,0},{2,3},{3,2},{4,5},{5,4},{6,7},{7,6},{8,9},{9,8},{10,11... | collective-permute-start | bytes 172040 | tf_op jit(solution)/shard_map/ppermute | solution.py:20
  68.0 0.9 %collective-permute-done.6 = f32[14,1024]{1,0:T(8,128)S(1)} collective-permute-done((f32[14,1024]{1,0:T(8,128)S(1)}, f32[14,1024]{1,0:T(8,128)S(1)}, u32[]{:S(2)}, u32[]{:S(2)}) %collective-permute-start.6) | collective-permute-done | bytes 57376 | tf_op jit(solution)/shard_map/ppermute | solution.py:20
  68.9 1.3 %collective-permute-start.7 = (f32[14,1024]{1,0:T(8,128)S(1)}, f32[14,1024]{1,0:T(8,128)S(1)}, u32[]{:S(2)}, u32[]{:S(2)}) collective-permute-start(f32[14,1024]{1,0:T(8,128)S(1)} %fusion), channel_id=1, source_target_pairs={{0,2},{1,3},{2,0},{3,1},{4,6},{5,7},{6,4},{7,5},{8,10},{9,11},{10,... | collective-permute-start | bytes 172040 | tf_op jit(solution)/shard_map/ppermute | solution.py:20
  70.2 7.4 %back.1 = (f32[1024,512]{1,0:T(8,128)}, f32[1024,512]{1,0:T(8,128)}) custom-call(s32[3]{0:T(128)} %shift-right-arithmetic_and_fusion.bits_ref, f32[1024,512]{1,0:T(8,128)} %refs_0_.11, f32[1024,512]{1,0:T(8,128)} %refs_1_.11, f32[4,128,128]{2,1,0:T(8,128)} %copy-done.1, f32[2,128,128]{2,1,0:T(8,128)} %copy-done.3, ...), custom_call_target="tpu_custom_call", output_to_operand_aliasing={{0}: (8, {}), {1}: (9, {})} | custom-call | flops 1000000000 | bytes 12582912 | tf_op jit(solution)/shard_map/back/pallas_call | solution.py:373
  77.6 0.0 collective-permute-done.7
  77.6 0.6 add.15
  (3 shorter events, 0.1 us)
Async XLA Ops:
  10.2 8.3 %collective-permute-start.1 = (f32[2,2,128,128]{3,2,1,0:T(8,128)}, f32[2,2,128,128]{3,2,1,0:T(8,128)S(1)}, u32[]{:S(2)}, u32[]{:S(2)}) collective-permute-start(f32[2,2,128,128]{3,2,1,0:T(8,128)} %get-tuple-element.33), channel_id=1, source_target_pairs={{0,4},{4,0},{8,12},{12,8},{16,20},{20,16},{24,28},{28,24},{1,5},{5... | collective-permute-start | bytes 786440 | tf_op jit(solution)/shard_map/ppermute | solution.py:20
  19.5 6.7 %collective-permute-start.2 = (f32[2,2,128,128]{3,2,1,0:T(8,128)S(1)}, f32[2,2,128,128]{3,2,1,0:T(8,128)S(1)}, u32[]{:S(2)}, u32[]{:S(2)}) collective-permute-start(f32[2,2,128,128]{3,2,1,0:T(8,128)S(1)} %add.12), channel_id=1, source_target_pairs={{0,8},{4,12},{8,0},{12,4},{16,24},{20,28},{24,16},{28,20},{1,9},{5... | collective-permute-start | bytes 786440 | tf_op jit(solution)/shard_map/ppermute | solution.py:20
  20.8 34.9 %collective-permute-start = (f32[4,128,128]{2,1,0:T(8,128)}, f32[4,128,128]{2,1,0:T(8,128)S(1)}, u32[]{:S(2)}, u32[]{:S(2)}) collective-permute-start(f32[4,128,128]{2,1,0:T(8,128)} %get-tuple-element.31), channel_id=1, source_target_pairs={{0,4},{4,0},{8,12},{12,8},{16,20},{20,16},{24,28},{28,24},{1,5},{5... | collective-permute-start | bytes 786440 | tf_op jit(solution)/shard_map/ppermute | solution.py:20
  26.2 14.8 %copy-start = (f32[2,128,128]{2,1,0:T(8,128)}, f32[2,128,128]{2,1,0:T(8,128)S(1)}, u32[]{:S(2)}) copy-start(f32[2,128,128]{2,1,0:T(8,128)S(1)} %get-tuple-element.59.refs_5_.refs_4_) | copy-start | bytes 393220
  26.2 16.0 %collective-permute-start.4 = (f32[1,2,128,128]{3,2,1,0:T(8,128)S(1)}, f32[1,2,128,128]{3,2,1,0:T(8,128)S(1)}, u32[]{:S(2)}, u32[]{:S(2)}) collective-permute-start(f32[1,2,128,128]{3,2,1,0:T(8,128)S(1)} %get-tuple-element.58), channel_id=1, source_target_pairs={{0,16},{4,20},{8,24},{12,28},{16,0},{20,4},{24,8},{28,12},{1,17},{... | collective-permute-start | bytes 393224 | tf_op jit(solution)/shard_map/ppermute | solution.py:20
  41.0 14.8 %collective-permute-start.3 = (f32[2,128,128]{2,1,0:T(8,128)S(1)}, f32[2,128,128]{2,1,0:T(8,128)S(1)}, u32[]{:S(2)}, u32[]{:S(2)}) collective-permute-start(f32[2,128,128]{2,1,0:T(8,128)S(1)} %get-tuple-element.59.refs_5_.refs_4_), channel_id=1, source_target_pairs={{0,4},{4,0},{8,12},{12,8},{16,20},{20,16},{24,28},{28,24},{1,5},{5... | collective-permute-start | bytes 393224 | tf_op jit(solution)/shard_map/ppermute | solution.py:20
  42.2 6.7 %copy-start.2 = (f32[1,2,128,128]{3,2,1,0:T(8,128)}, f32[1,2,128,128]{3,2,1,0:T(8,128)S(1)}, u32[]{:S(2)}) copy-start(f32[1,2,128,128]{3,2,1,0:T(8,128)S(1)} %collective-permute-done.4) | copy-start | bytes 393220
  42.2 13.6 %collective-permute-start.5 = (f32[2,128,128]{2,1,0:T(8,128)S(1)}, f32[2,128,128]{2,1,0:T(8,128)S(1)}, u32[]{:S(2)}, u32[]{:S(2)}) collective-permute-start(f32[2,128,128]{2,1,0:T(8,128)S(1)} %bitcast.4), channel_id=1, source_target_pairs={{0,4},{4,0},{8,12},{12,8},{16,20},{20,16},{24,28},{28,24},{1,5},{5... | collective-permute-start | bytes 393224 | tf_op jit(solution)/shard_map/ppermute | solution.py:20
  55.8 0.7 copy-start.1
  55.8 0.7 copy-start.3
  55.8 0.8 copy-start.4
  56.6 8.1 %copy-start.5 = (f32[16,1024]{1,0:T(8,128)S(1)}, f32[16,1024]{1,0:T(8,128)}, u32[]{:S(2)}) copy-start(f32[16,1024]{1,0:T(8,128)} %get-tuple-element.56) | copy-start | bytes 196612
  64.7 4.2 %collective-permute-start.6 = (f32[14,1024]{1,0:T(8,128)S(1)}, f32[14,1024]{1,0:T(8,128)S(1)}, u32[]{:S(2)}, u32[]{:S(2)}) collective-permute-start(f32[14,1024]{1,0:T(8,128)S(1)} %pad_maximum_fusion), channel_id=1, source_target_pairs={{0,1},{1,0},{2,3},{3,2},{4,5},{5,4},{6,7},{7,6},{8,9},{9,8},{10,11... | collective-permute-start | bytes 172040 | tf_op jit(solution)/shard_map/ppermute | solution.py:20
  68.9 8.7 %collective-permute-start.7 = (f32[14,1024]{1,0:T(8,128)S(1)}, f32[14,1024]{1,0:T(8,128)S(1)}, u32[]{:S(2)}, u32[]{:S(2)}) collective-permute-start(f32[14,1024]{1,0:T(8,128)S(1)} %fusion), channel_id=1, source_target_pairs={{0,2},{1,3},{2,0},{3,1},{4,6},{5,7},{6,4},{7,5},{8,10},{9,11},{10,... | collective-permute-start | bytes 172040 | tf_op jit(solution)/shard_map/ppermute | solution.py:20

commit v2 on v1

v2 whole, which is shorter than its diff:
```python
import functools

import jax
import jax.numpy as jnp
from jax import lax
from jax.experimental import pallas as pl
from jax.experimental.pallas import tpu as pltpu
from jax.sharding import PartitionSpec as P


DK = 128
C = 128
B = 256
SUB = 8
NN = (((1,), (0,)), ((), ()))
NT = (((1,), (1,)), ((), ()))
TN = (((0,), (0,)), ((), ()))


def partner(array, axis, stride):
    return lax.ppermute(array, axis, [(i, i ^ 1 << stride) for i in range(lax.axis_size(axis))])


def split(x):
    hi = x.astype(jnp.bfloat16)
    return hi, (x - hi.astype(jnp.float32)).astype(jnp.bfloat16)


def wide(parts):
    return jnp.concatenate(parts, axis=1)


def tall(parts):
    return jnp.concatenate(parts, axis=0)


def dot(a, b, dims):
    return lax.dot_general(a, b, dims, preferred_element_type=jnp.float32)


def halves(x):
    n = x.shape[1] // 2
    return x[:, :n] + x[:, n:]


def nn(a, b):
    right = wide(b)
    return halves(dot(wide(a), tall((right, right)), NN))


def nt(a, b):
    return halves(dot(wide(a), tall((wide((b[0], b[0])), wide((b[1], b[1])))), NT))


def tn(a, b):
    right = wide(b)
    return halves(dot(tall(a), tall((right, right)), TN))


def fold(x):
    return jnp.sum(x.reshape(x.shape[0] // SUB, SUB, x.shape[1]), axis=0)


def level_table():
    s = lax.broadcasted_iota(jnp.int32, (C, C), 0)
    t = lax.broadcasted_iota(jnp.int32, (C, C), 1)
    x = jnp.bitwise_xor(s, t)
    level = jnp.zeros((C, C), jnp.int32)
    for height in range(C.bit_length() - 1):
        level = level + (x >= 1 << height).astype(jnp.int32)
    return jnp.where(s <= t, level, -1)


def head_order(i, own, heads):
    return (i + (1 - own) * (heads // 2)) % heads


def state_kernel(first, bits_ref, q_ref, k_ref, v_ref, d_ref, w_ref, near_ref, send_ref, keep_ref, mix_ref, left_ref, right_ref, turned_ref, sum_ref):
    step = pl.program_id(0)
    heads = pl.num_programs(0)
    half = heads // 2
    head = head_order(step, bits_ref[0], heads)
    levels = send_ref.shape[0] + 1
    frames = q_ref.shape[0]
    chunks, inner = mix_ref.shape[0], C.bit_length()

    @pl.when(step == 0)
    def _():
        table = level_table()
        for c in range(chunks):
            mixing = jnp.zeros((C, C), jnp.float32)
            for level in range(inner):
                mixing = jnp.where(table == level, w_ref[level : level + 1, c * C : (c + 1) * C], mixing)
            mix_ref[c] = mixing

    for b in range(frames // B):
        span = slice(b * B, (b + 1) * B)
        k, q = k_ref[span, :], q_ref[span, :]
        left_ref[0, head, span, :] = wide(split(k))
        left_ref[1, head, span, :] = wide(split(q))
        right_ref[0, head, span, :] = wide(split(v_ref[span, :]))
        right_ref[1, head, span, :] = wide(split(d_ref[span, :]))
        turned_ref[0, head, :, span] = k.T
        turned_ref[1, head, :, span] = q.T
        for level in range(levels):
            bit = bits_ref[level]
            row = jnp.where(bit == 1, w_ref[first + level : first + level + 1, span], 1.0)
            grown = wide(split(row * turned_ref[bit, head, :, span]))
            right = right_ref[bit, head, span, :]
            term = dot(grown, tall((right, right)), NN)
            sum_ref[level] = term if b == 0 else sum_ref[level] + term
    near_ref[0] = halves(sum_ref[0])

    @pl.when(step < half)
    def _():
        for level in range(1, levels):
            send_ref[level - 1, 0] = halves(sum_ref[level])

    @pl.when(step >= half)
    def _():
        for level in range(1, levels):
            keep_ref[level - 1, 0] = halves(sum_ref[level])


def upper_pairs(chunks):
    heights = chunks.bit_length() - 1
    return [(c, k) for c in range(chunks) for k in range(heights) if c >> k & 1]


def parts(ref, *at):
    x = ref[at]
    return x[:, :DK], x[:, DK:]


def local_kernel(head, last, left_ref, right_ref, turned_ref, w_ref, mix_ref, *refs):
    if head:
        refs = refs[5:]
    qg_ref, kg_ref, vg_ref, pr_ref, wc_ref = refs[:5]
    frames = left_ref.shape[2]
    chunks = frames // C
    heights = chunks.bit_length() - 1
    inner = C.bit_length()
    pairs = upper_pairs(chunks)
    spans = [slice(c * C, (c + 1) * C) for c in range(chunks)]
    lanes = slice(head * DK, (head + 1) * DK)

    def add(ref, at, value):
        ref[at] = ref[at] + value if head else value

    sums = {}
    for c in range(chunks - 1):
        sums[c, 0] = tn(parts(left_ref, 0, head, spans[c]), parts(right_ref, 0, head, spans[c]))
    for k in range(1, heights):
        for b in range(chunks >> k):
            if b << k < chunks - (1 << k):
                sums[b, k] = sums[2 * b, k - 1] + sums[2 * b + 1, k - 1]

    def scores(c):
        ks, qs = parts(left_ref, 0, head, spans[c]), parts(left_ref, 1, head, spans[c])
        vs, ds = parts(right_ref, 0, head, spans[c]), parts(right_ref, 1, head, spans[c])
        gt = nt(ks, qs)
        et = nt(vs, ds)
        add(pr_ref, c, gt * et)
        mt = mix_ref[c]
        return split(mt * et), split(mt * gt)

    back = {}

    def gradients(c, me, mg):
        ks, qs = parts(left_ref, 0, head, spans[c]), parts(left_ref, 1, head, spans[c])
        vs, ds = parts(right_ref, 0, head, spans[c]), parts(right_ref, 1, head, spans[c])
        kg, vg, qg = nn(me, qs), nn(mg, ds), tn(me, ks)
        if c < chunks - 1:
            total = None
            for k in range(heights):
                if not c >> k & 1:
                    term = back[c >> k, k]
                    total = term if total is None else total + term
            bs = split(total)
            kg = kg + nt(vs, bs)
            vg = vg + nn(ks, bs)
        kg_ref[spans[c], lanes] = kg
        vg_ref[spans[c], lanes] = vg
        ups = [k for k in range(heights) if c >> k & 1]
        if ups:
            qt = turned_ref[1, head, :, spans[c]]
            mixed = None
            for k in ups:
                row = w_ref[inner + k : inner + k + 1, spans[c]]
                along = nt(split(sums[(c >> k) - 1, k]), ds)
                add(wc_ref, pairs.index((c, k)), fold(qt * along))
                term = row * along
                mixed = term if mixed is None else mixed + term
                grad = nn(split(row * qt), ds)
                key = ((c >> k) - 1, k)
                back[key] = back[key] + grad if key in back else grad
            qg = qg + mixed.T
        qg_ref[spans[c], lanes] = qg

    waiting = None
    for c in reversed(range(chunks)):
        now = scores(c)
        if waiting is not None:
            gradients(c + 1, *waiting)
        waiting = now
    gradients(0, *waiting)

    if last:
        wg_ref = refs[-1]
        table = level_table()
        wg_ref[...] = jnp.zeros_like(wg_ref)
        for c in range(chunks):
            product = pr_ref[c]
            for level in range(inner):
                row = jnp.sum(jnp.where(table == level, product, 0.0), axis=0, keepdims=True)
                wg_ref[level : level + 1, spans[c]] = row
        for i, (c, k) in enumerate(pairs):
            wg_ref[inner + k : inner + k + 1, spans[c]] = jnp.sum(wc_ref[i], axis=0, keepdims=True)


def received(refs, levels):
    step = pl.program_id(0)
    half = pl.num_programs(0) // 2
    found = [refs[0][0]]
    for level in range(1, levels):
        found.append(jnp.where(step < half, refs[2 * level - 1][0], refs[2 * level][0]))
    return found


def coarse_kernel(first, levels, bits_ref, right_ref, turned_ref, w_ref, qg_ref, *refs):
    arrived = refs[: 2 * levels - 1]
    out_ref, wg_ref, wc_ref = refs[2 * levels - 1 :]
    step = pl.program_id(0)
    heads = pl.num_programs(0)
    head = head_order(step, bits_ref[0], heads)
    frames = qg_ref.shape[0]
    lanes = pl.ds(pl.multiple_of(head * DK, DK), DK)
    states = []
    for level, state in enumerate(received(arrived, levels)):
        states.append(split(jnp.where(bits_ref[level] == 1, state, 0.0)))
    left = tall([wide(s) for s in states])

    @pl.when(step == 0)
    def _():
        wc_ref[...] = jnp.zeros_like(wc_ref)

    for c in range(frames // C):
        span = slice(c * C, (c + 1) * C)
        dh, dl = parts(right_ref, 1, head, span)
        along = halves(dot(left, tall((wide((dh, dh)), wide((dl, dl)))), NT))
        qt = turned_ref[1, head, :, span]
        mixed = None
        for level in range(levels):
            part = along[level * DK : (level + 1) * DK, :]
            wc_ref[level, :, span] += fold(qt * part)
            term = w_ref[first + level : first + level + 1, span] * part
            mixed = term if mixed is None else mixed + term
        out_ref[span, :] = qg_ref[span, lanes] + mixed.T

    @pl.when(step == heads - 1)
    def _():
        wg_ref[...] = jnp.zeros_like(wg_ref)
        for level in range(levels):
            wg_ref[level : level + 1, :] = jnp.sum(wc_ref[level], axis=0, keepdims=True)


def back_kernel(levels, bits_ref, left_ref, right_ref, kg_ref, vg_ref, *refs):
    arrived = refs[: 2 * levels - 1]
    ko_ref, vo_ref = refs[2 * levels - 1 :]
    head = head_order(pl.program_id(0), bits_ref[0], pl.num_programs(0))
    lanes = pl.ds(pl.multiple_of(head * DK, DK), DK)
    total = None
    for level, state in enumerate(received(arrived, levels)):
        term = jnp.where(bits_ref[level] == 0, state, 0.0)
        total = term if total is None else total + term
    bs = split(total)
    for b in range(kg_ref.shape[0] // B):
        span = slice(b * B, (b + 1) * B)
        ko_ref[span, :] = kg_ref[span, lanes] + nt(parts(right_ref, 0, head, span), bs)
        vo_ref[span, :] = vg_ref[span, lanes] + nn(parts(left_ref, 0, head, span), bs)


def params(mib):
    return pltpu.CompilerParams(dimension_semantics=("arbitrary",), vmem_limit_bytes=mib * 2**20)


def cost(flops, size):
    return pl.CostEstimate(flops=flops, bytes_accessed=size, transcendentals=0)


def body(query_rows, key_rows, value_rows, out_grad, level_weights):
    frames, width = query_rows.shape
    heads = width // DK
    half = heads // 2
    levels = level_weights.shape[0]
    fine = frames.bit_length()
    device_levels = levels - fine
    far = device_levels - 1
    f32, bf16 = jnp.float32, jnp.bfloat16
    big = jax.ShapeDtypeStruct((frames, width), f32)
    fine_rows = -(-fine // SUB) * SUB
    coarse_rows = -(-device_levels // SUB) * SUB
    chunks = frames // C
    pairs = max(1, len(upper_pairs(chunks)))
    block = frames * width * 4
    device = lax.axis_index("tm")
    bits = jnp.bitwise_and(jnp.right_shift(device, jnp.arange(device_levels)), 1).astype(jnp.int32)
    inputs = [pltpu.with_memory_space_constraint(x, pltpu.HBM) for x in (query_rows, key_rows, value_rows, out_grad)]

    def whole(shape):
        return pl.BlockSpec(shape, lambda i, *s: (0,) * len(shape))

    here = pl.BlockSpec(memory_space=pltpu.VMEM)
    ordered = pl.BlockSpec((frames, DK), lambda i, b: (0, head_order(i, b[0], heads)))
    first_half = lambda i: jnp.minimum(i, half - 1)
    second_half = lambda i: jnp.maximum(i - half, 0)

    near, send, keep, mix, left, right, turned = pl.pallas_call(
        functools.partial(state_kernel, fine),
        grid_spec=pltpu.PrefetchScalarGridSpec(
            num_scalar_prefetch=1,
            grid=(heads,),
            in_specs=[ordered] * 4 + [whole((levels, frames))],
            out_specs=[
                pl.BlockSpec((1, DK, DK), lambda i, b: (head_order(i, b[0], heads), 0, 0)),
                pl.BlockSpec((far, 1, DK, DK), lambda i, b: (0, first_half(i), 0, 0)),
                pl.BlockSpec((far, 1, DK, DK), lambda i, b: (0, second_half(i), 0, 0)),
                here,
                here,
                here,
                here,
            ],
            scratch_shapes=[pltpu.VMEM((device_levels, DK, 2 * DK), f32)],
        ),
        out_shape=[
            jax.ShapeDtypeStruct((heads, DK, DK), f32),
            jax.ShapeDtypeStruct((far, half, DK, DK), f32),
            jax.ShapeDtypeStruct((far, half, DK, DK), f32),
            pltpu.VMEM((chunks, C, C), f32),
            pltpu.VMEM((2, heads, frames, 2 * DK), bf16),
            pltpu.VMEM((2, heads, frames, 2 * DK), bf16),
            pltpu.VMEM((2, heads, DK, frames), f32),
        ],
        compiler_params=params(16),
        cost_estimate=cost(10**9, 4 * block),
        name="states",
    )(bits, *inputs, level_weights)

    inner = None
    for head in range(heads):
        last = head == heads - 1
        shapes = [pltpu.VMEM((frames, width), f32)] * 3
        shapes += [pltpu.VMEM((chunks, C, C), f32), pltpu.VMEM((pairs, SUB, C), f32)]
        inner = pl.pallas_call(
            functools.partial(local_kernel, head, last),
            in_specs=[here] * (10 if head else 5),
            out_specs=[here] * (6 if last else 5),
            out_shape=shapes + ([jax.ShapeDtypeStruct((fine_rows, frames), f32)] if last else []),
            input_output_aliases={5 + i: i for i in range(5)} if head else {},
            compiler_params=pltpu.CompilerParams(vmem_limit_bytes=16 * 2**20),
            cost_estimate=cost(10**9, 7 * block // heads),
        )(left, right, turned, level_weights, mix, *(inner or []))
    q_local, k_local, v_local, _, _, w_fine = inner

    arrived = []
    carried = keep + partner(send, "tm", 0)
    for height in range(1, device_levels):
        other = partner(carried, "tm", height)
        arrived.append(other[0])
        carried = carried[1:] + other[1:]
    states = [partner(near, "tm", 0)]
    for height in range(far):
        states += [partner(arrived[height], "tm", 0), arrived[height]]

    state_specs = [pl.BlockSpec((1, DK, DK), lambda i, b: (head_order(i, b[0], heads), 0, 0))]
    for _ in range(far):
        state_specs.append(pl.BlockSpec((1, DK, DK), lambda i, b: (first_half(i), 0, 0)))
        state_specs.append(pl.BlockSpec((1, DK, DK), lambda i, b: (second_half(i), 0, 0)))

    q_total, w_coarse = pl.pallas_call(
        functools.partial(coarse_kernel, fine, device_levels),
        grid_spec=pltpu.PrefetchScalarGridSpec(
            num_scalar_prefetch=1,
            grid=(heads,),
            in_specs=[here] * 4 + state_specs,
            out_specs=[ordered, whole((coarse_rows, frames))],
            scratch_shapes=[pltpu.VMEM((device_levels, SUB, frames), f32)],
        ),
        out_shape=[big, jax.ShapeDtypeStruct((coarse_rows, frames), f32)],
        compiler_params=params(16),
        cost_estimate=cost(10**9, 4 * block),
        name="coarse",
    )(bits, right, turned, level_weights, q_local, *states)

    weight_grad = jnp.concatenate([w_fine[:fine], w_coarse[:device_levels]], axis=0)
    for height in range(lax.axis_size("head").bit_length() - 1):
        weight_grad = weight_grad + partner(weight_grad, "head", height)

    k_total, v_total = pl.pallas_call(
        functools.partial(back_kernel, device_levels),
        grid_spec=pltpu.PrefetchScalarGridSpec(
            num_scalar_prefetch=1,
            grid=(heads,),
            in_specs=[here] * 4 + state_specs,
            out_specs=[ordered] * 2,
        ),
        out_shape=[big] * 2,
        compiler_params=params(16),
        cost_estimate=cost(10**9, 6 * block),
        name="back",
    )(bits, left, right, k_local, v_local, *states)
    return (q_total, k_total, v_total, weight_grad)


def solution(mesh):
    in_specs = (P("tm", "head"), P("tm", "head"), P("tm", "head"), P("tm", "head"), P(None, "tm"))
    out_specs = (P("tm", "head"), P("tm", "head"), P("tm", "head"), P(None, "tm"))
    return jax.shard_map(body, mesh=mesh, in_specs=in_specs, out_specs=out_specs, check_vma=False)
```

time: 79.5 us -> 53.5 us (0.67)
  Pallas kernels: 49.7 us -> 26.5 us
  other arithmetic: 2.26 us -> 0.72 us
    pallas_call x4, Pallas kernels: 26 us -> 10.7 us  [body(): pl.pallas_call(functools.partial(local_kernel, head, last), in_specs=[her...]
    pallas_call x1, Pallas kernels: 7.4 us -> 3.96 us  [body(): pl.pallas_call(functools.partial(back_kernel, device_levels), grid_spec=p...]
    pallas_call x1, Pallas kernels: 7.38 us -> 4.45 us  [body(): pl.pallas_call(functools.partial(coarse_kernel, fine, device_levels), gri...]
    pallas_call x1, Pallas kernels: 8.97 us -> 7.35 us  [body(): pl.pallas_call(functools.partial(state_kernel, fine), grid_spec=pltpu.Pre...]
    add x1, other arithmetic: 0.99 us -> 0.03 us  [body(): carried = keep + partner(send, 'tm', 0)]
  transfers between devices with their start and end apart: 8 -> 8, of which waited for: 3 -> 3; matrix products, arithmetic and copies ran while one was open for 0% -> 0% of each run, Pallas kernels for 43% -> 28%
where the time goes in v2:
time: 53.5 us; the launch traced here: 52.7 us
  Pallas kernels  26.5 us (50%)
  starting transfers between devices  12.9 us (24%)
  waiting for transfers between devices  11 us (21%)
  local copies, waits for them, and re-layouts  0.84 us (2%)
  other arithmetic  0.72 us (1%)
  between operations  0.72 us (1%)
    ppermute x8, starting transfers between devices, partner(): lax.ppermute(array, axis, [(i, i ^ 1 << stride) for i in range(lax.axis_s...  12.9 us
    ppermute x8, waiting for transfers between devices, partner(): lax.ppermute(array, axis, [(i, i ^ 1 << stride) for i in range(lax.axis_s...  11 us
    pallas_call x4, Pallas kernels, body(): pl.pallas_call(functools.partial(local_kernel, head, last), in_specs=[her...  10.7 us
    pallas_call x1, Pallas kernels, body(): pl.pallas_call(functools.partial(state_kernel, fine), grid_spec=pltpu.Pre...  7.35 us
    pallas_call x1, Pallas kernels, body(): pl.pallas_call(functools.partial(coarse_kernel, fine, device_levels), gri...  4.45 us
    pallas_call x1, Pallas kernels, body(): pl.pallas_call(functools.partial(back_kernel, device_levels), grid_spec=p...  3.96 us
  transfers between devices with their start and end apart: 8, of which 3 were waited for; matrix products, arithmetic and copies ran while one was open for 0% of the time, Pallas kernels for 28%

profile of v2, /device:TPU:1, one launch (start us, length us, event | category | flops | bytes accessed | tf_op | source)
XLA Modules:
  0.0 52.7 jit_solution(8871136363107154219)
XLA Ops:
  0.6 0.0 copy-start
  0.7 0.8 %copy-done = f32[14,1024]{1,0:T(8,128)S(1)} copy-done((f32[14,1024]{1,0:T(8,128)S(1)}, f32[14,1024]{1,0:T(8,128)}, u32[]{:S(2)}) %copy-start) | copy-done | bytes 57368
  1.5 0.0 copy-start.1
  1.5 7.4 %states.1 = (f32[4,128,128]{2,1,0:T(8,128)S(1)}, f32[2,2,128,128]{3,2,1,0:T(8,128)S(1)}, f32[2,2,128,128]{3,2,1,0:T(8,128)S(1)}, f32[8,128,128]{2,1,0:T(8,128)S(...) custom-call(s32[3]{0:T(128)S(1)} %shift-right-arithmetic_and_fusion., ...), custom_call_target="tpu_custom_call" | custom-call | flops 1000000000 | bytes 8388608 | tf_op jit(solution)/shard_map/states/pallas_call | solution.py:318
  8.9 2.1 %collective-permute-start.1 = (f32[2,2,128,128]{3,2,1,0:T(8,128)S(1)}, f32[2,2,128,128]{3,2,1,0:T(8,128)S(1)}, u32[]{:S(2)}, u32[]{:S(2)}) collective-permute-start(f32[2,2,128,128]{3,2,1,0:T(8,128)S(1)} %get-tuple-element.56), channel_id=1, source_target_pairs={{0,4},{4,0},{8,12},{12,8},{16,20},{20,16},{24,28},{28,24},{1,5},{5... | collective-permute-start | bytes 786440 | tf_op jit(solution)/shard_map/ppermute | solution.py:21
  10.9 6.0 %collective-permute-done.1 = f32[2,2,128,128]{3,2,1,0:T(8,128)S(1)} collective-permute-done((f32[2,2,128,128]{3,2,1,0:T(8,128)S(1)}, f32[2,2,128,128]{3,2,1,0:T(8,128)S(1)}, u32[]{:S(2)}, u32[]{:S(2)}) %collective-permute-start.1) | collective-permute-done | bytes 262176 | tf_op jit(solution)/shard_map/ppermute | solution.py:21
  17.0 1.3 %collective-permute-start.2 = (f32[2,2,128,128]{3,2,1,0:T(8,128)S(1)}, f32[2,2,128,128]{3,2,1,0:T(8,128)S(1)}, u32[]{:S(2)}, u32[]{:S(2)}) collective-permute-start(f32[2,2,128,128]{3,2,1,0:T(8,128)S(1)} %add.12), channel_id=1, source_target_pairs={{0,8},{4,12},{8,0},{12,4},{16,24},{20,28},{24,16},{28,20},{1,9},{5... | collective-permute-start | bytes 786440 | tf_op jit(solution)/shard_map/ppermute | solution.py:21
  18.3 1.2 %collective-permute-start = (f32[4,128,128]{2,1,0:T(8,128)S(1)}, f32[4,128,128]{2,1,0:T(8,128)S(1)}, u32[]{:S(2)}, u32[]{:S(2)}) collective-permute-start(f32[4,128,128]{2,1,0:T(8,128)S(1)} %get-tuple-element.54), channel_id=1, source_target_pairs={{0,4},{4,0},{8,12},{12,8},{16,20},{20,16},{24,28},{28,24},{1,5},{5... | collective-permute-start | bytes 786440 | tf_op jit(solution)/shard_map/ppermute | solution.py:21
  19.6 4.1 %collective-permute-done.2 = f32[2,2,128,128]{3,2,1,0:T(8,128)S(1)} collective-permute-done((f32[2,2,128,128]{3,2,1,0:T(8,128)S(1)}, f32[2,2,128,128]{3,2,1,0:T(8,128)S(1)}, u32[]{:S(2)}, u32[]{:S(2)}) %collective-permute-start.2) | collective-permute-done | bytes 262176 | tf_op jit(solution)/shard_map/ppermute | solution.py:21
  23.7 2.0 %collective-permute-start.4 = (f32[1,2,128,128]{3,2,1,0:T(8,128)S(1)}, f32[1,2,128,128]{3,2,1,0:T(8,128)S(1)}, u32[]{:S(2)}, u32[]{:S(2)}) collective-permute-start(f32[1,2,128,128]{3,2,1,0:T(8,128)S(1)} %get-tuple-element.64), channel_id=1, source_target_pairs={{0,16},{4,20},{8,24},{12,28},{16,0},{20,4},{24,8},{28,12},{1,17},{... | collective-permute-start | bytes 393224 | tf_op jit(solution)/shard_map/ppermute | solution.py:21
  25.7 0.0 copy-done.1
  25.7 2.7 %shard_map.84 = (f32[1024,512]{1,0:T(8,128)S(1)}, f32[1024,512]{1,0:T(8,128)S(1)}, f32[1024,512]{1,0:T(8,128)S(1)}, f32[8,128,128]{2,1,0:T(8,128)S(1)}, f32[12,8,128]{2,1,0:T(8,128)S(1)}) custom-call(bf16[2,4,1024,256]{3,2,1,0:T(8,128)(2,1)S(1)} %get-tuple-element.36.left_ref, bf16[2,4,1024,256]{3,2,1,0:T(8,128)(2,1)S(1)} %get-tuple-element.34.right_ref, ...), custom_call_target="tpu_custom_call" | custom-call | flops 1000000000 | bytes 3670016 | tf_op jit(solution)/shard_map/pallas_call | solution.py:354
  28.4 2.7 %shard_map.85 = (f32[1024,512]{1,0:T(8,128)S(1)}, f32[1024,512]{1,0:T(8,128)S(1)}, f32[1024,512]{1,0:T(8,128)S(1)}, f32[8,128,128]{2,1,0:T(8,128)S(1)}, f32[12,8,128]{2,1,0:T(8,128)S(1)}) custom-call(bf16[2,4,1024,256]{3,2,1,0:T(8,128)(2,1)S(1)} %get-tuple-element.36.left_ref, ...), custom_call_target="tpu_custom_call", output_to_operand_aliasing={{0}: (5, {}), {1}: (6, {}), {2}: (7, {}), {3}: (8, {}), {4}... | custom-call | flops 1000000000 | bytes 3670016 | tf_op jit(solution)/shard_map/pallas_call | solution.py:354
  31.0 1.4 %collective-permute-start.3 = (f32[2,128,128]{2,1,0:T(8,128)S(1)}, f32[2,128,128]{2,1,0:T(8,128)S(1)}, u32[]{:S(2)}, u32[]{:S(2)}) collective-permute-start(f32[2,128,128]{2,1,0:T(8,128)S(1)} %get-tuple-element.65.refs_2_), channel_id=1, source_target_pairs={{0,4},{4,0},{8,12},{12,8},{16,20},{20,16},{24,28},{28,24},{1,5},{5... | collective-permute-start | bytes 393224 | tf_op jit(solution)/shard_map/ppermute | solution.py:21
  32.4 0.0 collective-permute-done.4
  32.4 0.1 collective-permute-start.5
  32.6 2.7 %shard_map.86 = (f32[1024,512]{1,0:T(8,128)S(1)}, f32[1024,512]{1,0:T(8,128)S(1)}, f32[1024,512]{1,0:T(8,128)S(1)}, f32[8,128,128]{2,1,0:T(8,128)S(1)}, f32[12,8,128]{2,1,0:T(8,128)S(1)}) custom-call(bf16[2,4,1024,256]{3,2,1,0:T(8,128)(2,1)S(1)} %get-tuple-element.36.left_ref, ...), custom_call_target="tpu_custom_call", output_to_operand_aliasing={{0}: (5, {}), {1}: (6, {}), {2}: (7, {}), {3}: (8, {}), {4}... | custom-call | flops 1000000000 | bytes 3670016 | tf_op jit(solution)/shard_map/pallas_call | solution.py:354
  35.2 2.7 %shard_map.87 = (f32[1024,512]{1,0:T(8,128)S(1)}, f32[1024,512]{1,0:T(8,128)S(1)}, f32[1024,512]{1,0:T(8,128)S(1)}, f32[8,128,128]{2,1,0:T(8,128)S(1)}, f32[12,8...) custom-call(bf16[2,4,1024,256]{3,2,1,0:T(8,128)(2,1)S(1)} %get-tuple, ...), custom_call_target="tpu_custom_call", output_to_operand_aliasing={{0}: (5, {}), {1}: (6, {}), {2}: (7, {}), {3}: (8, {}), {4}... | custom-call | flops 1000000000 | bytes 3670016 | tf_op jit(solution)/shard_map/pallas_call | solution.py:354
  38.0 0.0 collective-permute-done.refs_0_
  38.0 0.0 collective-permute-done.3.refs_1_
  38.0 0.0 collective-permute-done.5.refs_3_
  38.0 4.4 %coarse.1 = (f32[1024,512]{1,0:T(8,128)}, f32[8,1024]{1,0:T(8,128)S(1)}) custom-call(s32[3]{0:T(128)S(1)} %shift-right-arithmetic_and_fusion.bits_ref, bf16[2,4,1024,256]{3,2,1,0:T(8,128)(2,1)S(1)} %get-tuple-element.34.right_ref, f32[2,4,128,1024]{3,2,1,0:T(8,128)S(1)} %get-tuple-element.35.turned_ref, f32[14,1024]{1,0:T(8,128)S(1)} %copy-done.1, ...), custom_call_target="tpu_custom_call" | custom-call | flops 1000000000 | bytes 8388608 | tf_op jit(solution)/shard_map/coarse/pallas_call | solution.py:380
  42.5 3.3 %collective-permute-start.6 = (f32[14,1024]{1,0:T(8,128)S(1)}, f32[14,1024]{1,0:T(8,128)S(1)}, u32[]{:S(2)}, u32[]{:S(2)}) collective-permute-start(f32[14,1024]{1,0:T(8,128)S(1)} %pad_maximum_fusion), channel_id=1, source_target_pairs={{0,1},{1,0},{2,3},{3,2},{4,5},{5,4},{6,7},{7,6},{8,9},{9,8},{10,11... | collective-permute-start | bytes 172040 | tf_op jit(solution)/shard_map/ppermute | solution.py:21
  45.8 0.9 %collective-permute-done.6 = f32[14,1024]{1,0:T(8,128)S(1)} collective-permute-done((f32[14,1024]{1,0:T(8,128)S(1)}, f32[14,1024]{1,0:T(8,128)S(1)}, u32[]{:S(2)}, u32[]{:S(2)}) %collective-permute-start.6) | collective-permute-done | bytes 57376 | tf_op jit(solution)/shard_map/ppermute | solution.py:21
  46.7 1.4 %collective-permute-start.7 = (f32[14,1024]{1,0:T(8,128)S(1)}, f32[14,1024]{1,0:T(8,128)S(1)}, u32[]{:S(2)}, u32[]{:S(2)}) collective-permute-start(f32[14,1024]{1,0:T(8,128)S(1)} %fusion), channel_id=1, source_target_pairs={{0,2},{1,3},{2,0},{3,1},{4,6},{5,7},{6,4},{7,5},{8,10},{9,11},{10,... | collective-permute-start | bytes 172040 | tf_op jit(solution)/shard_map/ppermute | solution.py:21
  48.1 4.0 %back.1 = (f32[1024,512]{1,0:T(8,128)}, f32[1024,512]{1,0:T(8,128)}) custom-call(s32[3]{0:T(128)S(1)} %shift-right-arithmetic_and_fusion.bits_ref, bf16[2,4,1024,256]{3,2,1,0:T(8,128)(2,1)S(1)} %get-tuple-element.36.left_ref, bf16[2,4,1024,256]{3,2,1,0:T(8,128)(2,1)S(1)} %get-tuple-element.34.right_ref, f32[1024,512]{1,0:T(8,128)S(1)} %get-tuple-element.58.kg_ref, ...), custom_call_target="tpu_custom_call" | custom-call | flops 1000000000 | bytes 12582912 | tf_op jit(solution)/shard_map/back/pallas_call | solution.py:399
  52.0 0.0 collective-permute-done.7
  52.0 0.6 %add.15 = f32[14,1024]{1,0:T(8,128)} add(f32[14,1024]{1,0:T(8,128)S(1)} %fusion, f32[14,1024]{1,0:T(8,128)S(1)} %collective-permute-done.7) | non-fusion elementwise | flops 14336 | bytes 172032 | tf_op jit(solution)/shard_map/add | solution.py:397
  (6 shorter events, 0.1 us)
Async XLA Ops:
  0.6 0.8 %copy-start = (f32[14,1024]{1,0:T(8,128)S(1)}, f32[14,1024]{1,0:T(8,128)}, u32[]{:S(2)}) copy-start(f32[14,1024]{1,0:T(8,128)} %w_ref.11) | copy-start | bytes 172036
  1.5 24.2 %copy-start.1 = (f32[14,1024]{1,0:T(8,128)S(1)}, f32[14,1024]{1,0:T(8,128)}, u32[]{:S(2)}) copy-start(f32[14,1024]{1,0:T(8,128)} %w_ref.11) | copy-start | bytes 172036
  8.9 8.1 %collective-permute-start.1 = (f32[2,2,128,128]{3,2,1,0:T(8,128)S(1)}, f32[2,2,128,128]{3,2,1,0:T(8,128)S(1)}, u32[]{:S(2)}, u32[]{:S(2)}) collective-permute-start(f32[2,2,128,128]{3,2,1,0:T(8,128)S(1)} %get-tuple-element.56), channel_id=1, source_target_pairs={{0,4},{4,0},{8,12},{12,8},{16,20},{20,16},{24,28},{28,24},{1,5},{5... | collective-permute-start | bytes 786440 | tf_op jit(solution)/shard_map/ppermute | solution.py:21
  17.0 6.7 %collective-permute-start.2 = (f32[2,2,128,128]{3,2,1,0:T(8,128)S(1)}, f32[2,2,128,128]{3,2,1,0:T(8,128)S(1)}, u32[]{:S(2)}, u32[]{:S(2)}) collective-permute-start(f32[2,2,128,128]{3,2,1,0:T(8,128)S(1)} %add.12), channel_id=1, source_target_pairs={{0,8},{4,12},{8,0},{12,4},{16,24},{20,28},{24,16},{28,20},{1,9},{5... | collective-permute-start | bytes 786440 | tf_op jit(solution)/shard_map/ppermute | solution.py:21
  18.3 19.7 %collective-permute-start = (f32[4,128,128]{2,1,0:T(8,128)S(1)}, f32[4,128,128]{2,1,0:T(8,128)S(1)}, u32[]{:S(2)}, u32[]{:S(2)}) collective-permute-start(f32[4,128,128]{2,1,0:T(8,128)S(1)} %get-tuple-element.54), channel_id=1, source_target_pairs={{0,4},{4,0},{8,12},{12,8},{16,20},{20,16},{24,28},{28,24},{1,5},{5... | collective-permute-start | bytes 786440 | tf_op jit(solution)/shard_map/ppermute | solution.py:21
  23.7 8.8 %collective-permute-start.4 = (f32[1,2,128,128]{3,2,1,0:T(8,128)S(1)}, f32[1,2,128,128]{3,2,1,0:T(8,128)S(1)}, u32[]{:S(2)}, u32[]{:S(2)}) collective-permute-start(f32[1,2,128,128]{3,2,1,0:T(8,128)S(1)} %get-tuple-element.64), channel_id=1, source_target_pairs={{0,16},{4,20},{8,24},{12,28},{16,0},{20,4},{24,8},{28,12},{1,17},{... | collective-permute-start | bytes 393224 | tf_op jit(solution)/shard_map/ppermute | solution.py:21
  31.0 7.0 %collective-permute-start.3 = (f32[2,128,128]{2,1,0:T(8,128)S(1)}, f32[2,128,128]{2,1,0:T(8,128)S(1)}, u32[]{:S(2)}, u32[]{:S(2)}) collective-permute-start(f32[2,128,128]{2,1,0:T(8,128)S(1)} %get-tuple-element.65.refs_2_), channel_id=1, source_target_pairs={{0,4},{4,0},{8,12},{12,8},{16,20},{20,16},{24,28},{28,24},{1,5},{5... | collective-permute-start | bytes 393224 | tf_op jit(solution)/shard_map/ppermute | solution.py:21
  32.4 5.6 %collective-permute-start.5 = (f32[2,128,128]{2,1,0:T(8,128)S(1)}, f32[2,128,128]{2,1,0:T(8,128)S(1)}, u32[]{:S(2)}, u32[]{:S(2)}) collective-permute-start(f32[2,128,128]{2,1,0:T(8,128)S(1)} %bitcast.4), channel_id=1, source_target_pairs={{0,4},{4,0},{8,12},{12,8},{16,20},{20,16},{24,28},{28,24},{1,5},{5... | collective-permute-start | bytes 393224 | tf_op jit(solution)/shard_map/ppermute | solution.py:21
  42.5 4.2 %collective-permute-start.6 = (f32[14,1024]{1,0:T(8,128)S(1)}, f32[14,1024]{1,0:T(8,128)S(1)}, u32[]{:S(2)}, u32[]{:S(2)}) collective-permute-start(f32[14,1024]{1,0:T(8,128)S(1)} %pad_maximum_fusion), channel_id=1, source_target_pairs={{0,1},{1,0},{2,3},{3,2},{4,5},{5,4},{6,7},{7,6},{8,9},{9,8},{10,11... | collective-permute-start | bytes 172040 | tf_op jit(solution)/shard_map/ppermute | solution.py:21
  46.7 5.3 %collective-permute-start.7 = (f32[14,1024]{1,0:T(8,128)S(1)}, f32[14,1024]{1,0:T(8,128)S(1)}, u32[]{:S(2)}, u32[]{:S(2)}) collective-permute-start(f32[14,1024]{1,0:T(8,128)S(1)} %fusion), channel_id=1, source_target_pairs={{0,2},{1,3},{2,0},{3,1},{4,6},{5,7},{6,4},{7,5},{8,10},{9,11},{10,... | collective-permute-start | bytes 172040 | tf_op jit(solution)/shard_map/ppermute | solution.py:21
